TPU v7x, 512 devices: a whole 4x8x8 slice. The times are simulated.
512 devices in a mesh: term: 8 (over z), sector: 64 (over x, y, core).
Axes of the slice: x: 4, y: 8, z: 8, core: 2. Of those that a mesh axis runs over, the one named last changes fastest.
Arguments:
- wave_tiles: bfloat16 [1024, 2, 128, 128], P('sector'), may hold values from -6 to 6
- left_env: bfloat16 [8, 64, 128, 128], P('term', 'sector'), may hold values from -0.5 to 0.5
- right_env: bfloat16 [8, 64, 128, 128], P('term', 'sector'), may hold values from -0.5 to 0.5
- send_list: int32 [64, 128], P('sector'), may hold values from -1 to 15, as said below
- left_tasks: int32 [8, 64, 96, 3], P('term', 'sector'), may hold values from 0 to 127, as said below
- right_tasks: int32 [8, 64, 256, 3], P('term', 'sector'), may hold values from 0 to 63, as said below
Outputs:
- sigma: float32 [1024, 2, 128, 128], P('sector', None, 'term')
Inputs may be any that keep to these rules, and one draw needn't show every extreme that they name: send_list[s, o * 2 + c] is a tile index local to sender s, or -1 for an empty slot; some owner drawn from the seed receives a full 2 tiles from every sender. `left_tasks`: entries 0, 1, 2 lie below 64, 128 and 32. `right_tasks`: entries 0, 1, 2 lie below 32, 64 and 16.
All inputs are finite; a program needn't handle non-finite values.
Results may differ from a plain program's by a relative error of at most 0.0029.
Values may be sent and summed in bfloat16 or wider, within the bound.
A program may use at most 128 MiB of HBM per device.

v0:
```python
import math

import jax
import jax.numpy as jnp
from jax import lax
from jax.sharding import PartitionSpec as P

INTER_TILES = 32


def run_tasks(tasks, first_tiles, second_tiles, contract, count):
    block = math.gcd(tasks.shape[0], 32)
    shape = (count,) + tuple(contract(first_tiles[:1], second_tiles[:1]).shape[1:])

    def step(turn, total):
        rows = lax.dynamic_slice_in_dim(tasks, turn * block, block, 0)
        first = jnp.take(first_tiles, rows[:, 0], axis=0)
        second = jnp.take(second_tiles, rows[:, 1], axis=0)
        return total.at[rows[:, 2]].add(contract(first, second))

    return lax.fori_loop(0, tasks.shape[0] // block, step, jnp.zeros(shape, jnp.float32))


def left_product(env_part, wave_part):
    return jnp.einsum("bij,bvjk->bvik", env_part, wave_part, preferred_element_type=jnp.float32)


def right_product(inter_part, env_part):
    return jnp.einsum("bvij,bjk->bvik", inter_part, env_part, preferred_element_type=jnp.float32)


def shards(wave_tiles, left_env, right_env, send_list, left_tasks, right_tasks):
    env_left, env_right = (
        lax.all_gather(left_env, "sector", axis=1, tiled=True),
        lax.all_gather(right_env, "sector", axis=1, tiled=True),
    )
    env_left = env_left[0]
    env_right = env_right[0]
    slot_list = send_list[0]
    live = slot_list >= 0
    picked = jnp.take(wave_tiles, jnp.maximum(slot_list, 0), axis=0)
    outgoing = jnp.where(live[:, None, None, None], picked, jnp.zeros((), jnp.bfloat16))
    tile_dim = wave_tiles.shape[2]
    groups = lax.axis_size("term")
    share = tile_dim // groups
    received = lax.all_to_all(outgoing, "sector", split_axis=0, concat_axis=0, tiled=True)
    inter = run_tasks(left_tasks[0, 0], env_left, received, left_product, INTER_TILES).astype(
        jnp.bfloat16
    )
    partial_value = run_tasks(
        right_tasks[0, 0], inter, env_right, right_product, wave_tiles.shape[0]
    )
    summed = lax.psum(partial_value, "term")
    return lax.dynamic_slice_in_dim(summed, lax.axis_index("term") * share, share, 2)


def solution(mesh):
    in_specs = (
        P("sector", None, None, None),
        P("term", "sector", None, None),
        P("term", "sector", None, None),
        P("sector", None),
        P("term", "sector", None, None),
        P("term", "sector", None, None),
    )
    out_specs = P("sector", None, "term", None)
    return jax.shard_map(shards, mesh=mesh, in_specs=in_specs, out_specs=out_specs, check_vma=False)
```

profile of v0, /device:TPU:7, one launch (start us, length us, event | category | flops | bytes accessed | tf_op | source)
XLA Modules:
  0.0 559.5 jit_solution(14975568767976974510)
XLA Ops:
  8.0 6.5 %gather_fusion.4 = bf16[128,2,128,128]{3,2,1,0:T(8,128)(2,1)} fusion(bf16[16,2,128,128]{3,2,1,0:T(8,128)(2,1)S(1)} %copy-done, s32[1024]{0:T(1024)S(1)} %pad_clamp_fusion.4), kind=kCustom, calls=%fused_computation.4 | custom fusion | bytes 16777728 | tf_op jit(solution)/shard_map/jit(_take)/gather | solution.py:41
  14.5 7.5 %select_select_fusion = bf16[128,2,128,128]{3,2,1,0:T(8,128)(2,1)} fusion(bf16[128,2,128,128]{3,2,1,0:T(8,128)(2,1)} %gather_fusion.4, pred[128]{0:T(512)(128)(4,1)S(1)} %get-tuple-element.225, pred[128]{0:T(512)(128)(4,1)S(1)} %get-tuple-element.224), kind=kLoop, calls=%fused_computation.45 | loop fusion | flops 8388608 | bytes 16777472 | tf_op jit(solution)/shard_map/jit(_where)/select_n | solution.py:42
  22.0 11.7 %all-to-all-start = ((bf16[128,2,128,128]{3,2,1,0:T(8,128)(2,1)}), bf16[128,2,128,128]{3,2,1,0:T(8,128)(2,1)}, u32[]{:S(2)}, u32[]{:S(2)}) async-start(bf16[128,2,128,128]{3,2,1,0:T(8,128)(2,1)} %select_select_fusion), calls=%async_computation | async-start | bytes 16777216 | tf_op jit(solution)/shard_map/all_to_all | solution.py:46
  35.3 103.7 %all-gather.3.cloned.1.call-done = bf16[1,64,128,128]{3,2,0,1:T(8,128)(2,1)} async-done(((bf16[1,1,128,128]{3,2,0,1:T(8,128)(2,1)}), bf16[1,64,128,128]{3,2,0,1:T(8,128)(2,1)}) %all-gather.3.cloned.1.call-update) | async-done | bytes 2097168 | tf_op jit(solution)/shard_map/all_gather | solution.py:34
  139.0 91.5 %all-to-all-done = bf16[128,2,128,128]{3,2,1,0:T(8,128)(2,1)} async-done(((bf16[128,2,128,128]{3,2,1,0:T(8,128)(2,1)}), bf16[128,2,128,128]{3,2,1,0:T(8,128)(2,1)}, u32[]{:S(2)}, u32[]{:S(2)}) %all-to-all-start) | async-done | bytes 8388640 | tf_op jit(solution)/shard_map/all_to_all | solution.py:46
  232.9 82.2 %while.26 = (s32[]{:T(128)}, f32[32,2,128,128]{3,2,1,0:T(8,128)}, s32[96,3]{0,1:T(4,128)S(1)}, bf16[128,2,128,128]{3,2,1,0:T(8,128)(2,1)}, bf16[64,128,128]{2,1,...) while((s32[]{:T(128)}, f32[32,2,128,128]{3,2,1,0:T(8,128)}, s32[96,3]{0,1:T(4,128)S(1)}, ...), condition=%wide.region_2.4_spmd, body=%wide.region_0.3_spmd.sunk | while | flops 271059520 | bytes 34613776 | solution.py:21
  244.7 5.6 %copy.23 = f32[32,2,128,128]{3,2,1,0:T(8,128)} copy(f32[32,2,128,128]{2,3,1,0:T(8,128)} %convolution_bitcast_fusion.2) | data formatting | bytes 8388608 | tf_op jit(solution)/shard_map/while/body/eval_jaxpr/bij,bvjk->bvik/transpose | solution.py:25
  250.3 9.9 %scatter_fusion = f32[32,2,128,128]{3,2,1,0:T(8,128)} fusion(f32[32,2,128,128]{3,2,1,0:T(8,128)} %get-tuple-element.314, s32[32]{0:T(128)S(1)} %get-tuple-element.291, f32[32,2,128,128]{3,2,1,0:T(8,128)} %copy.23), kind=kCustom, calls=%fused_computation.5.clone.1 | custom fusion | flops 1048576 | bytes 12583040 | tf_op jit(solution)/shard_map/while/body/eval_jaxpr/scatter-add | solution.py:19
  272.1 5.6 %copy.23 = f32[32,2,128,128]{3,2,1,0:T(8,128)} copy(f32[32,2,128,128]{2,3,1,0:T(8,128)} %convolution_bitcast_fusion.2) | data formatting | bytes 8388608 | tf_op jit(solution)/shard_map/while/body/eval_jaxpr/bij,bvjk->bvik/transpose | solution.py:25
  277.7 10.0 %scatter_fusion = f32[32,2,128,128]{3,2,1,0:T(8,128)} fusion(f32[32,2,128,128]{3,2,1,0:T(8,128)} %get-tuple-element.314, s32[32]{0:T(128)S(1)} %get-tuple-element.291, f32[32,2,128,128]{3,2,1,0:T(8,128)} %copy.23), kind=kCustom, calls=%fused_computation.5.clone.1 | custom fusion | flops 1048576 | bytes 12583040 | tf_op jit(solution)/shard_map/while/body/eval_jaxpr/scatter-add | solution.py:19
  299.6 5.6 %copy.23 = f32[32,2,128,128]{3,2,1,0:T(8,128)} copy(f32[32,2,128,128]{2,3,1,0:T(8,128)} %convolution_bitcast_fusion.2) | data formatting | bytes 8388608 | tf_op jit(solution)/shard_map/while/body/eval_jaxpr/bij,bvjk->bvik/transpose | solution.py:25
  305.2 9.9 %scatter_fusion = f32[32,2,128,128]{3,2,1,0:T(8,128)} fusion(f32[32,2,128,128]{3,2,1,0:T(8,128)} %get-tuple-element.314, s32[32]{0:T(128)S(1)} %get-tuple-element.291, f32[32,2,128,128]{3,2,1,0:T(8,128)} %copy.23), kind=kCustom, calls=%fused_computation.5.clone.1 | custom fusion | flops 1048576 | bytes 12583040 | tf_op jit(solution)/shard_map/while/body/eval_jaxpr/scatter-add | solution.py:19
  319.2 145.2 %while.27 = (s32[]{:T(128)}, f32[16,2,128,128]{3,2,1,0:T(8,128)S(1)}, s32[256,3]{0,1:T(4,128)S(1)}, bf16[32,2,128,128]{3,2,1,0:T(8,128)(2,1)}, bf16[64,128,128]{...) while((s32[]{:T(128)}, f32[16,2,128,128]{3,2,1,0:T(8,128)S(1)}, ...), condition=%wide.region_5.7_spmd, body=%wide.region_3.6_spmd.sunk | while | flops 271059520 | bytes 26225168 | solution.py:21
  330.9 6.5 %scatter_fusion.1 = f32[16,2,128,128]{3,2,1,0:T(8,128)S(1)} fusion(f32[16,2,128,128]{3,2,1,0:T(8,128)S(1)} %get-tuple-element.341, s32[32]{0:T(128)S(1)} %get-tuple-element.300, f32[32,2,128,128]{3,2,1,0:T(8,128)} %fusion.34), kind=kCustom, calls=%fused_computation.6.clone.1 | custom fusion | flops 1048576 | bytes 12583040 | tf_op jit(solution)/shard_map/while/body/eval_jaxpr/scatter-add | solution.py:19
  344.5 4.6 fusion.34
  349.1 6.5 %scatter_fusion.1 = f32[16,2,128,128]{3,2,1,0:T(8,128)S(1)} fusion(f32[16,2,128,128]{3,2,1,0:T(8,128)S(1)} %get-tuple-element.341, s32[32]{0:T(128)S(1)} %get-tuple-element.300, f32[32,2,128,128]{3,2,1,0:T(8,128)} %fusion.34), kind=kCustom, calls=%fused_computation.6.clone.1 | custom fusion | flops 1048576 | bytes 12583040 | tf_op jit(solution)/shard_map/while/body/eval_jaxpr/scatter-add | solution.py:19
  367.2 6.5 %scatter_fusion.1 = f32[16,2,128,128]{3,2,1,0:T(8,128)S(1)} fusion(f32[16,2,128,128]{3,2,1,0:T(8,128)S(1)} %get-tuple-element.341, s32[32]{0:T(128)S(1)} %get-tuple-element.300, f32[32,2,128,128]{3,2,1,0:T(8,128)} %fusion.34), kind=kCustom, calls=%fused_computation.6.clone.1 | custom fusion | flops 1048576 | bytes 12583040 | tf_op jit(solution)/shard_map/while/body/eval_jaxpr/scatter-add | solution.py:19
  380.8 4.6 fusion.34
  385.4 6.5 %scatter_fusion.1 = f32[16,2,128,128]{3,2,1,0:T(8,128)S(1)} fusion(f32[16,2,128,128]{3,2,1,0:T(8,128)S(1)} %get-tuple-element.341, s32[32]{0:T(128)S(1)} %get-tuple-element.300, f32[32,2,128,128]{3,2,1,0:T(8,128)} %fusion.34), kind=kCustom, calls=%fused_computation.6.clone.1 | custom fusion | flops 1048576 | bytes 12583040 | tf_op jit(solution)/shard_map/while/body/eval_jaxpr/scatter-add | solution.py:19
  403.5 6.5 %scatter_fusion.1 = f32[16,2,128,128]{3,2,1,0:T(8,128)S(1)} fusion(f32[16,2,128,128]{3,2,1,0:T(8,128)S(1)} %get-tuple-element.341, s32[32]{0:T(128)S(1)} %get-tuple-element.300, f32[32,2,128,128]{3,2,1,0:T(8,128)} %fusion.34), kind=kCustom, calls=%fused_computation.6.clone.1 | custom fusion | flops 1048576 | bytes 12583040 | tf_op jit(solution)/shard_map/while/body/eval_jaxpr/scatter-add | solution.py:19
  421.7 6.5 %scatter_fusion.1 = f32[16,2,128,128]{3,2,1,0:T(8,128)S(1)} fusion(f32[16,2,128,128]{3,2,1,0:T(8,128)S(1)} %get-tuple-element.341, s32[32]{0:T(128)S(1)} %get-tuple-element.300, f32[32,2,128,128]{3,2,1,0:T(8,128)} %fusion.34), kind=kCustom, calls=%fused_computation.6.clone.1 | custom fusion | flops 1048576 | bytes 12583040 | tf_op jit(solution)/shard_map/while/body/eval_jaxpr/scatter-add | solution.py:19
  439.8 6.5 %scatter_fusion.1 = f32[16,2,128,128]{3,2,1,0:T(8,128)S(1)} fusion(f32[16,2,128,128]{3,2,1,0:T(8,128)S(1)} %get-tuple-element.341, s32[32]{0:T(128)S(1)} %get-tuple-element.300, f32[32,2,128,128]{3,2,1,0:T(8,128)} %fusion.34), kind=kCustom, calls=%fused_computation.6.clone.1 | custom fusion | flops 1048576 | bytes 12583040 | tf_op jit(solution)/shard_map/while/body/eval_jaxpr/scatter-add | solution.py:19
  458.0 6.5 %scatter_fusion.1 = f32[16,2,128,128]{3,2,1,0:T(8,128)S(1)} fusion(f32[16,2,128,128]{3,2,1,0:T(8,128)S(1)} %get-tuple-element.341, s32[32]{0:T(128)S(1)} %get-tuple-element.300, f32[32,2,128,128]{3,2,1,0:T(8,128)} %fusion.34), kind=kCustom, calls=%fused_computation.6.clone.1 | custom fusion | flops 1048576 | bytes 12583040 | tf_op jit(solution)/shard_map/while/body/eval_jaxpr/scatter-add | solution.py:19
  465.8 85.5 %all-reduce.2.cloned.1.call-done = f32[16,2,128,128]{3,2,1,0:T(8,128)} async-done(((f32[16,2,128,128]{3,2,1,0:T(8,128)}), f32[16,2,128,128]{3,2,1,0:T(8,128)}) %all-reduce.2.cloned.1.call-update) | async-done | bytes 2097168 | tf_op jit(solution)/shard_map/psum | solution.py:53
  (121 shorter events, 131.9 us)
Async XLA Ops:
  6.5 1.4 copy-start
  22.0 13.3 %copy-start.3 = (s32[1,1,96,3]{2,1,3,0:T(1,128)S(1)}, s32[1,1,96,3]{2,1,3,0:T(1,128)}, u32[]{:S(2)}) copy-start(s32[1,1,96,3]{2,1,3,0:T(1,128)} %param.16) | copy-start | bytes 3460
  22.0 13.3 %copy-start.2 = (s32[1,1,256,3]{2,1,3,0:T(1,128)S(1)}, s32[1,1,256,3]{2,1,3,0:T(1,128)}, u32[]{:S(2)}) copy-start(s32[1,1,256,3]{2,1,3,0:T(1,128)} %param.17) | copy-start | bytes 9220
  22.0 208.4 %all-to-all-start = ((bf16[128,2,128,128]{3,2,1,0:T(8,128)(2,1)}), bf16[128,2,128,128]{3,2,1,0:T(8,128)(2,1)}, u32[]{:S(2)}, u32[]{:S(2)}) async-start(bf16[128,2,128,128]{3,2,1,0:T(8,128)(2,1)} %select_select_fusion), calls=%async_computation | async-start | bytes 16777216 | tf_op jit(solution)/shard_map/all_to_all | solution.py:46
  33.8 105.2 %all-gather.3.cloned.1.call-start = ((), (), s32[]{:S(2)}) async-start(), calls=%async_computation.1 | async-start | bytes 2129920 | tf_op jit(solution)/shard_map/all_gather | solution.py:34
  34.5 284.5 %all-gather.5.cloned.1.call-start = ((), (), s32[]{:S(2)}) async-start(), calls=%async_computation.2 | async-start | bytes 2129920 | tf_op jit(solution)/shard_map/all_gather | solution.py:35
  35.2 516.0 %all-reduce.2.cloned.1.call-start = ((), (), s32[]{:S(2)}) async-start(), calls=%async_computation.3 | async-start | bytes 4194304 | tf_op jit(solution)/shard_map/psum | solution.py:53
  464.5 1.3 copy-start.1
Sparse Core Ops, SparseCore 0:
  38.0 100.9 all-gather.2
  142.3 94.3 all-gather.4
  465.9 85.2 all-reduce.1
where the time goes:
time: 565 us; the launch traced here: 559 us
  waiting for transfers between devices  282 us (50%)
  local copies, waits for them, and re-layouts  108 us (19%)
  other arithmetic  94.9 us (17%)
  matrix products  48.7 us (9%)
  between operations  13.2 us (2%)
  starting transfers between devices  11.9 us (2%)
    all_gather x1, waiting for transfers between devices, shards(): lax.all_gather(left_env, 'sector', axis=1, tiled=True)  104 us
    all_to_all x1, waiting for transfers between devices, shards(): lax.all_to_all(outgoing, 'sector', split_axis=0, concat_axis=0, tiled=True)  91.5 us
    psum x1, waiting for transfers between devices, shards(): summed = lax.psum(partial_value, 'term')  85.5 us
    scatter-add x11, other arithmetic, step(): return total.at[rows[:, 2]].add(contract(first, second))  81.7 us
    gather x11, local copies, waits for them, and re-layouts, step(): first = jnp.take(first_tiles, rows[:, 0], axis=0)  39.7 us
    gather x11, local copies, waits for them, and re-layouts, step(): second = jnp.take(second_tiles, rows[:, 1], axis=0)  38.9 us
    dot_general x8, matrix products, right_product(): jnp.einsum('bvij,bjk->bvik', inter_part, env_part, preferred_element_type...  36.6 us
    transpose x3, local copies, waits for them, and re-layouts, left_product(): jnp.einsum('bij,bvjk->bvik', env_part, wave_part, preferred_element_type=...  16.9 us
  transfers between devices with their start and end apart: 4, of which 3 were waited for; matrix products, arithmetic and copies ran while one was open for 16% of the time, Pallas kernels for 0%

commit v1 on v0

v1 whole, which is shorter than its diff:
```python
import functools

import jax
import jax.numpy as jnp
from jax import lax
from jax.experimental import pallas as pl
from jax.experimental.pallas import tpu as pltpu
from jax.sharding import Mesh
from jax.sharding import PartitionSpec as P

INTER_TILES = 32
TILES = 16
LEFT = 96
RIGHT = 256
AXES = ("z", "x", "y", "core")
SWAP = []
for _z in range(8):
    for _x in range(4):
        for _y in range(8):
            for _c in range(2):
                source = ((_z * 4 + _x) * 8 + _y) * 2 + _c
                target = (((2 * _x + _c) * 4 + _z // 2) * 8 + _y) * 2 + _z % 2
                SWAP.append((source, target))


def tasks_kernel(ltask, rtask, wave_ref, left_ref, right_ref, out_ref, acc, inter, total):
    acc[...] = jnp.zeros_like(acc)
    total[...] = jnp.zeros_like(total)

    def left_step(t, carry):
        e, s, x = ltask[3 * t], ltask[3 * t + 1], ltask[3 * t + 2]
        rhs = jnp.concatenate([wave_ref[s, 0], wave_ref[s, 1]], axis=1)
        acc[x] += jnp.dot(left_ref[e], rhs, preferred_element_type=jnp.float32)
        return carry

    lax.fori_loop(0, LEFT, left_step, 0, unroll=4)
    for v in range(2):
        inter[:, v] = acc[:, :, 128 * v : 128 * (v + 1)].astype(jnp.bfloat16)

    def right_step(t, carry):
        x, e, k = rtask[3 * t], rtask[3 * t + 1], rtask[3 * t + 2]
        lhs = inter[x].reshape(256, 128)
        total[k] += jnp.dot(lhs, right_ref[e], preferred_element_type=jnp.float32)
        return carry

    lax.fori_loop(0, RIGHT, right_step, 0, unroll=4)
    for k in range(TILES):
        out_ref[:, k] = jnp.swapaxes(total[k].reshape(2, 8, 16, 128), 0, 1)


def run_tasks(ltask, rtask, wave, left, right):
    vmem = pl.BlockSpec(memory_space=pltpu.VMEM)
    smem = pl.BlockSpec(memory_space=pltpu.SMEM)
    return pl.pallas_call(
        tasks_kernel,
        out_shape=jax.ShapeDtypeStruct((8, TILES, 2, 16, 128), jnp.float32),
        in_specs=[smem, smem, vmem, vmem, vmem],
        out_specs=vmem,
        scratch_shapes=[
            pltpu.VMEM((INTER_TILES, 128, 256), jnp.float32),
            pltpu.VMEM((INTER_TILES, 2, 128, 128), jnp.bfloat16),
            pltpu.VMEM((TILES, 256, 128), jnp.float32),
        ],
        compiler_params=pltpu.CompilerParams(vmem_limit_bytes=44 << 20),
        name="tasks",
    )(ltask, rtask, wave, left, right)


def shards(wave_tiles, left_env, right_env, send_list, left_tasks, right_tasks):
    z = lax.axis_index("z")
    left_rows, right_rows = left_tasks[0, 0], right_tasks[0, 0]
    env_place = lambda e: (((e >> 1) & 7) << 3) | ((e >> 4) << 1) | (e & 1)
    slot = left_rows[:, 1]
    sender = slot >> 1
    place = ((((sender >> 4) << 1) | (sender & 1)) << 4) | (((sender >> 1) & 7) << 1) | (slot & 1)
    left_rows = jnp.stack([env_place(left_rows[:, 0]), place, left_rows[:, 2]], axis=1)
    right_rows = jnp.stack(
        [right_rows[:, 0], env_place(right_rows[:, 1]), right_rows[:, 2]], axis=1
    )
    rows = jnp.concatenate([left_rows, right_rows], axis=0).reshape(-1)
    rows = lax.ppermute(rows, AXES, SWAP)
    ltask, rtask = rows[: 3 * LEFT], rows[3 * LEFT :]

    env = jnp.stack([left_env[0, 0], right_env[0, 0]])
    env = lax.ppermute(env, AXES, SWAP)
    left = lax.all_gather(env[0], ("y", "z"), axis=0)
    right = lax.all_gather(env[1], ("y", "z"), axis=0)

    chosen = lax.dynamic_index_in_dim(send_list.reshape(4, 8, 2, 2), z // 2, 0, False)
    chosen = lax.dynamic_index_in_dim(chosen, z % 2, 1, False).reshape(16)
    picked = jnp.take(wave_tiles, jnp.maximum(chosen, 0), axis=0)
    outgoing = jnp.where((chosen >= 0)[:, None, None, None], picked, jnp.zeros((), jnp.bfloat16))
    arrived = lax.all_to_all(outgoing, "y", split_axis=0, concat_axis=0, tiled=True)
    wave = lax.all_gather(arrived, ("x", "core"), axis=0, tiled=True)

    partial = run_tasks(ltask, rtask, wave, left, right)
    summed = lax.psum_scatter(partial, ("x", "core"), scatter_dimension=0, tiled=False)
    return lax.ppermute(summed, AXES, SWAP)


def solution(mesh):
    fine = Mesh(mesh.devices.reshape(8, 4, 8, 2), AXES)
    sector = ("x", "y", "core")
    in_specs = (
        P(sector, None, None, None),
        P("z", sector, None, None),
        P("z", sector, None, None),
        P(sector, None),
        P("z", sector, None, None),
        P("z", sector, None, None),
    )
    out_specs = P(sector, None, "z", None)
    return jax.shard_map(shards, mesh=fine, in_specs=in_specs, out_specs=out_specs, check_vma=False)
```

time: 565 us -> 347 us (0.61)
  local copies, waits for them, and re-layouts: 108 us -> 6.65 us
  other arithmetic: 94.9 us -> 2.57 us
  matrix products: 48.7 us -> 0 us
  waiting for transfers between devices: 282 us -> 239 us
  blocking collectives: 0 us -> 36.9 us
  Pallas kernels: 0 us -> 26 us
  starting transfers between devices: 11.9 us -> 22.7 us
    all_to_all x1 -> x0, waiting for transfers between devices: 91.5 us -> none  [shards(): lax.all_to_all(outgoing, 'sector', split_axis=0, concat_axis=0, tiled=True)]
    psum x1 -> x0, waiting for transfers between devices: 85.5 us -> none  [shards(): summed = lax.psum(partial_value, 'term')]
    gather x23 -> x1, local copies, waits for them, and re-layouts: 85.2 us -> 0.75 us  [shards(): picked = jnp.take(wave_tiles, jnp.maximum(chosen, 0), axis=0)]
    scatter-add x11 -> x0, other arithmetic: 81.7 us -> none  [step(): return total.at[rows[:, 2]].add(contract(first, second))]
    all_gather x2 -> x3, waiting for transfers between devices: 104 us -> 172 us  [the longest x1 83.6 us: shards(): left = lax.all_gather(env[0], ('y', 'z'), axis=0)]
    dot_general x11 -> x0, matrix products: 48.7 us -> none  [the longest x8 36.6 us: right_product(): jnp.einsum('bvij,bjk->bvik', inter_part, env_part, preferred_element_type...]
    reduce_scatter x0 -> x1, waiting for transfers between devices: none -> 40.1 us  [shards(): lax.psum_scatter(partial, ('x', 'core'), scatter_dimension=0, tiled=False)]
    all_to_all x0 -> x1, blocking collectives: none -> 36.9 us  [shards(): lax.all_to_all(outgoing, 'y', split_axis=0, concat_axis=0, tiled=True)]
  transfers between devices with their start and end apart: 4 -> 7, of which waited for: 3 -> 7; matrix products, arithmetic and copies ran while one was open for 16% -> 1% of each run, Pallas kernels for 0% -> 0%
where the time goes in v1:
time: 347 us
  waiting for transfers between devices  239 us (69%)
  blocking collectives  36.9 us (11%)
  Pallas kernels  26 us (7%)
  starting transfers between devices  22.7 us (7%)
  between operations  13.3 us (4%)
  local copies, waits for them, and re-layouts  6.65 us (2%)
    all_gather x1, waiting for transfers between devices, shards(): left = lax.all_gather(env[0], ('y', 'z'), axis=0)  83.6 us
    all_gather x1, waiting for transfers between devices, shards(): wave = lax.all_gather(arrived, ('x', 'core'), axis=0, tiled=True)  56.5 us
    reduce_scatter x1, waiting for transfers between devices, shards(): lax.psum_scatter(partial, ('x', 'core'), scatter_dimension=0, tiled=False)  40.1 us
    all_to_all x1, blocking collectives, shards(): lax.all_to_all(outgoing, 'y', split_axis=0, concat_axis=0, tiled=True)  36.9 us
    all_gather x1, waiting for transfers between devices, shards(): right = lax.all_gather(env[1], ('y', 'z'), axis=0)  31.7 us
    pallas_call x1, Pallas kernels, run_tasks(): pl.pallas_call(tasks_kernel, out_shape=jax.ShapeDtypeStruct((8, TILES, 2,...  26 us
    ppermute x1, waiting for transfers between devices, shards(): return lax.ppermute(summed, AXES, SWAP)  17.9 us
    ppermute x1, starting transfers between devices, shards(): env = lax.ppermute(env, AXES, SWAP)  11.1 us
  transfers between devices with their start and end apart: 7, of which 7 were waited for; matrix products, arithmetic and copies ran while one was open for 1% of the time, Pallas kernels for 0%

profile of v1, /device:TPU:7, one launch (start us, length us, event | category | flops | bytes accessed | tf_op | source)
XLA Modules:
  0.0 346.8 jit_solution(2068814724286947738)
XLA Ops:
  6.5 0.9 pad_maximum_fusion
  7.4 11.1 %collective-permute-start.1 = (bf16[2,128,128]{2,1,0:T(8,128)(2,1)S(1)}, bf16[2,128,128]{2,1,0:T(8,128)(2,1)S(1)}, u32[]{:S(2)}, u32[]{:S(2)}) collective-permute-start(bf16[2,128,128]{2,1,0:T(8,128)(2,1)S(1)} %pad_maximum_fusion), channel_id=1, source_target_pairs={{0,0},{1,64},{2,2},{3,66},{4,4},{5,68},{6,6},{7,70},{8,8},{9,72},{... | collective-permute-start | bytes 196616 | tf_op jit(solution)/shard_map/ppermute | solution.py:85
  18.5 4.6 %collective-permute-done.1 = bf16[2,128,128]{2,1,0:T(8,128)(2,1)S(1)} collective-permute-done((bf16[2,128,128]{2,1,0:T(8,128)(2,1)S(1)}, bf16[2,128,128]{2,1,0:T(8,128)(2,1)S(1)}, u32[]{:S(2)}, u32[]{:S(2)}) %collective-permute-start.1) | collective-permute-done | bytes 65568 | tf_op jit(solution)/shard_map/ppermute | solution.py:85
  23.1 0.6 fusion.1
  23.8 0.7 all-gather.6.cloned.1.call-update
  24.6 0.5 broadcast.101
  25.1 1.3 reduce.11
  26.4 0.2 reshape.40
  27.0 0.7 gather_fusion
  27.7 0.2 select_select_fusion
  28.0 36.9 %all_to_all.5 = bf16[16,2,128,128]{3,2,1,0:T(8,128)(2,1)} all-to-all(bf16[16,2,128,128]{3,2,1,0:T(8,128)(2,1)S(1)} %select_select_fusion), channel_id=1, replica_groups=mesh['z'=8,'x'=4,'y'=8,'core'=2] {'y'}, dimensions={0} | all-to-all | bytes 2097152 | tf_op jit(solution)/shard_map/all_to_all | solution.py:93
  65.3 0.2 reshape.39
  65.5 4.8 %collective-permute-start = (s32[1056]{0:T(1024)S(1)}, s32[1056]{0:T(1024)S(1)}, u32[]{:S(2)}, u32[]{:S(2)}) collective-permute-start(s32[1056]{0:T(1024)S(1)} %reshape.39), channel_id=1, source_target_pairs={{0,0},{1,64},{2,2},{3,66},{4,4},{5,68},{6,6},{7,70},{8,8},{9,72},{... | collective-permute-start | bytes 12680 | tf_op jit(solution)/shard_map/ppermute | solution.py:81
  70.3 3.5 %collective-permute-done = s32[1056]{0:T(1024)S(1)} collective-permute-done((s32[1056]{0:T(1024)S(1)}, s32[1056]{0:T(1024)S(1)}, u32[]{:S(2)}, u32[]{:S(2)}) %collective-permute-start) | collective-permute-done | bytes 4256 | tf_op jit(solution)/shard_map/ppermute | solution.py:81
  73.9 31.7 %all-gather.8.cloned.1.call-done.right_ref = bf16[64,128,128]{2,1,0:T(8,128)(2,1)} async-done(((bf16[1,128,128]{2,1,0:T(8,128)(2,1)}), bf16[64,128,128]{2,1,0:T(8,128)(2,1)}) %all-gather.8.cloned.1.call-update) | async-done | bytes 2097168 | tf_op jit(solution)/shard_map/all_gather | solution.py:87
  105.6 83.6 %all-gather.6.cloned.1.call-done.left_ref = bf16[64,128,128]{2,1,0:T(8,128)(2,1)} async-done(((bf16[1,128,128]{2,1,0:T(8,128)(2,1)}), bf16[64,128,128]{2,1,0:T(8,128)(2,1)}) %all-gather.6.cloned.1.call-update) | async-done | bytes 2097168 | tf_op jit(solution)/shard_map/all_gather | solution.py:86
  189.1 56.5 %all-gather.4.cloned.1.call-done.wave_ref = bf16[128,2,128,128]{3,2,1,0:T(8,128)(2,1)} async-done(((bf16[16,2,128,128]{3,2,1,0:T(8,128)(2,1)}), bf16[128,2,128,128]{3,2,1,0:T(8,128)(2,1)}) %all-gather.4.cloned.1.call-update) | async-done | bytes 8388624 | tf_op jit(solution)/shard_map/all_gather | solution.py:94
  245.7 1.6 copy-done.1
  247.2 1.6 copy-done.2
  248.8 26.0 %tasks.1 = f32[8,16,2,16,128]{4,3,2,1,0:T(8,128)} custom-call(s32[288]{0:T(512)S(1)} %slice.45.ltask, s32[768]{0:T(1024)S(1)} %slice.46.rtask, bf16[128,2,128,128]{3,2,1,0:T(8,128)(2,1)} %all-gather.4.cloned.1.call-done.wave_ref, bf16[64,128,128]{2,1,0:T(8,128)(2,1)S(1)} %copy-done.2, bf16[64,128,128]{2,1,0:T(8,128)(2,1)S(1)} %copy-done.1), custom_call_target="tpu_custom_call" | custom-call | tf_op jit(solution)/shard_map/tasks/pallas_call | solution.py:54
  274.9 40.1 %reduce-scatter.2.cloned.1.call-done = f32[1,16,2,16,128]{4,3,2,1,0:T(8,128)} async-done(((f32[8,16,2,16,128]{4,3,2,1,0:T(8,128)}), f32[1,16,2,16,128]{4,3,2,1,0:T(8,128)}) %reduce-scatter.2.cloned.1.call-update) | async-done | bytes 262160 | tf_op jit(solution)/shard_map/reduce_scatter | solution.py:97
  315.0 6.7 %collective-permute-start.2 = (f32[16,2,16,128]{3,2,1,0:T(8,128)}, f32[16,2,16,128]{3,2,1,0:T(8,128)S(1)}, u32[]{:S(2)}, u32[]{:S(2)}) collective-permute-start(f32[16,2,16,128]{3,2,1,0:T(8,128)} %bitcast.13), channel_id=1, source_target_pairs={{0,0},{1,64},{2,2},{3,66},{4,4},{5,68},{6,6},{7,70},{8,8},{9,72},{... | collective-permute-start | bytes 786440 | tf_op jit(solution)/shard_map/ppermute | solution.py:98
  321.7 17.9 %collective-permute-done.2 = f32[16,2,16,128]{3,2,1,0:T(8,128)S(1)} collective-permute-done((f32[16,2,16,128]{3,2,1,0:T(8,128)}, f32[16,2,16,128]{3,2,1,0:T(8,128)S(1)}, u32[]{:S(2)}, u32[]{:S(2)}) %collective-permute-start.2) | collective-permute-done | bytes 262176 | tf_op jit(solution)/shard_map/ppermute | solution.py:98
  339.5 0.7 copy.16
  (29 shorter events, 0.8 us)
Async XLA Ops:
  6.5 20.4 %copy-start = (bf16[16,2,128,128]{3,2,1,0:T(8,128)(2,1)S(1)}, bf16[16,2,128,128]{3,2,1,0:T(8,128)(2,1)}, u32[]{:S(2)}) copy-start(bf16[16,2,128,128]{3,2,1,0:T(8,128)(2,1)} %param.6) | copy-start | bytes 3145732
  6.5 99.0 %all-gather.8.cloned.1.call-start = ((), (), s32[]{:S(2)}) async-start(), calls=%async_computation.4 | async-start | bytes 2129920 | tf_op jit(solution)/shard_map/all_gather | solution.py:87
  7.4 15.7 %collective-permute-start.1 = (bf16[2,128,128]{2,1,0:T(8,128)(2,1)S(1)}, bf16[2,128,128]{2,1,0:T(8,128)(2,1)S(1)}, u32[]{:S(2)}, u32[]{:S(2)}) collective-permute-start(bf16[2,128,128]{2,1,0:T(8,128)(2,1)S(1)} %pad_maximum_fusion), channel_id=1, source_target_pairs={{0,0},{1,64},{2,2},{3,66},{4,4},{5,68},{6,6},{7,70},{8,8},{9,72},{... | collective-permute-start | bytes 196616 | tf_op jit(solution)/shard_map/ppermute | solution.py:85
  23.8 165.4 %all-gather.6.cloned.1.call-start = ((), (), s32[]{:S(2)}) async-start(), calls=%async_computation.3 | async-start | bytes 2129920 | tf_op jit(solution)/shard_map/all_gather | solution.py:86
  24.5 221.1 %all-gather.4.cloned.1.call-start = ((), (), s32[]{:S(2)}) async-start(), calls=%async_computation.2 | async-start | bytes 9437184 | tf_op jit(solution)/shard_map/all_gather | solution.py:94
  28.0 37.0 %copy-start.4 = (s32[1,1,96,3]{2,1,3,0:T(1,128)S(1)}, s32[1,1,96,3]{2,1,3,0:T(1,128)}, u32[]{:S(2)}) copy-start(s32[1,1,96,3]{2,1,3,0:T(1,128)} %param.10) | copy-start | bytes 3460
  28.0 37.1 %copy-start.3 = (s32[1,1,256,3]{2,1,3,0:T(1,128)S(1)}, s32[1,1,256,3]{2,1,3,0:T(1,128)}, u32[]{:S(2)}) copy-start(s32[1,1,256,3]{2,1,3,0:T(1,128)} %param.11) | copy-start | bytes 9220
  65.0 250.0 %reduce-scatter.2.cloned.1.call-start = ((), (), s32[]{:S(2)}) async-start(), calls=%async_computation.5 | async-start | bytes 2359296 | tf_op jit(solution)/shard_map/reduce_scatter | solution.py:97
  65.5 8.3 %collective-permute-start = (s32[1056]{0:T(1024)S(1)}, s32[1056]{0:T(1024)S(1)}, u32[]{:S(2)}, u32[]{:S(2)}) collective-permute-start(s32[1056]{0:T(1024)S(1)} %reshape.39), channel_id=1, source_target_pairs={{0,0},{1,64},{2,2},{3,66},{4,4},{5,68},{6,6},{7,70},{8,8},{9,72},{... | collective-permute-start | bytes 12680 | tf_op jit(solution)/shard_map/ppermute | solution.py:81
  245.7 1.6 copy-start.1
  247.2 1.6 copy-start.2
  315.0 24.6 %collective-permute-start.2 = (f32[16,2,16,128]{3,2,1,0:T(8,128)}, f32[16,2,16,128]{3,2,1,0:T(8,128)S(1)}, u32[]{:S(2)}, u32[]{:S(2)}) collective-permute-start(f32[16,2,16,128]{3,2,1,0:T(8,128)} %bitcast.13), channel_id=1, source_target_pairs={{0,0},{1,64},{2,2},{3,66},{4,4},{5,68},{6,6},{7,70},{8,8},{9,72},{... | collective-permute-start | bytes 786440 | tf_op jit(solution)/shard_map/ppermute | solution.py:98
Sparse Core Ops, SparseCore 0:
  23.9 81.6 all-gather.7
  108.6 80.5 all-gather.5
  191.3 54.3 all-gather.3
  275.0 39.9 reduce-scatter.1

commit v2 on v1

v2 whole, which is shorter than its diff:
```python
import jax
import jax.numpy as jnp
from jax import lax
from jax.experimental import pallas as pl
from jax.experimental.pallas import tpu as pltpu
from jax.sharding import Mesh
from jax.sharding import PartitionSpec as P

INTER_TILES = 32
TILES = 16
LEFT = 96
RIGHT = 256
ROWS = 16
AXES = ("z", "x", "y", "core")
MESH = pl.DeviceIdType.MESH
ANY = pl.BlockSpec(memory_space=pl.ANY)
VMEM = pl.BlockSpec(memory_space=pltpu.VMEM)
SMEM = pl.BlockSpec(memory_space=pltpu.SMEM)


def place():
    return tuple(lax.axis_index(name) for name in AXES)


def swapped(z, x, y, c):
    return (2 * x + c, z // 2, y, z % 2)


def greet(peers, partner, fixed):
    barrier = pltpu.get_barrier_semaphore()
    for peer in peers:
        pl.semaphore_signal(barrier, inc=1, device_id=peer, device_id_type=MESH)

    @pl.when(jnp.logical_not(fixed))
    def _():
        pl.semaphore_signal(barrier, inc=1, device_id=partner, device_id_type=MESH)

    pl.semaphore_wait(barrier, len(peers) + jnp.where(fixed, 0, 1))


def gather_kernel(
    rows_in, left_in, right_in, outgoing, rows, env, wave,
    wrecv, erecv, mate_recv, rows_recv, send,
):
    z, x, y, c = place()
    xc = 2 * x + c
    fixed = z == xc
    partner = swapped(z, x, y, c)
    mate = (z, x, y, 1 - c)
    xup, xdown = (z, (x + 1) % 4, y, c), (z, (x + 3) % 4, y, c)
    zup, zdown = ((z + 1) % 8, x, y, c), ((z + 7) % 8, x, y, c)
    others = [(z, x, (y + d) % 8, c) for d in range(1, 8)]
    greet(others + [mate, xup, xdown, zup, zdown], partner, fixed)
    Y_SEND, EY_SEND, MATE_SEND, XUP, XDOWN, ZUP, ZDOWN, E_SEND, ROWS_SEND = range(9)

    def remote(source, target, sender, receiver, device):
        pltpu.make_async_remote_copy(
            src_ref=source, dst_ref=target, send_sem=send.at[sender], recv_sem=receiver,
            device_id=device, device_id_type=MESH,
        ).start()

    def wait(ref, sem):
        pltpu.make_async_copy(ref, ref, sem).wait()

    def pass_wave(slot, sender, device):
        remote(wave.at[slot], wave.at[slot], sender, wrecv.at[slot], device)

    def pass_mate(slot):
        remote(wave.at[slot], wave.at[slot], MATE_SEND, mate_recv, mate)

    def pass_env(slot, sender, device):
        remote(env.at[slot], env.at[slot], sender, erecv.at[slot], device)

    theirs = xc * 8 + y

    @pl.when(fixed)
    def _():
        pltpu.make_async_copy(left_in, env.at[theirs, 0], erecv.at[theirs]).start()
        pltpu.make_async_copy(right_in, env.at[theirs, 1], erecv.at[theirs]).start()
        pltpu.make_async_copy(rows_in, rows, rows_recv).start()

    @pl.when(jnp.logical_not(fixed))
    def _():
        remote(left_in, env.at[theirs, 0], E_SEND, erecv.at[theirs], partner)
        remote(right_in, env.at[theirs, 1], E_SEND, erecv.at[theirs], partner)
        remote(rows_in, rows, ROWS_SEND, rows_recv, partner)

    mine = xc * 8 + y
    pltpu.make_async_copy(outgoing.at[y], wave.at[mine], wrecv.at[mine]).start()
    for d in (1, 7):
        remote(outgoing.at[(y + d) % 8], wave.at[mine], Y_SEND, wrecv.at[mine], others[d - 1])
    own = z * 8 + y
    wait(env.at[own], erecv.at[own])
    for d in (1, 7, 2, 6, 3, 5, 4):
        pass_env(own, EY_SEND, others[d - 1])
    for d in (2, 6, 3, 5, 4):
        remote(outgoing.at[(y + d) % 8], wave.at[mine], Y_SEND, wrecv.at[mine], others[d - 1])

    def source(r):
        step = (r + 1) // 2
        return (y + jnp.where(r % 2 == 1, step, 8 - step)) % 8

    def turn(i, carry):
        @pl.when(i < 8)
        def _():
            yy = source(i)
            slot = xc * 8 + yy
            wait(wave.at[slot], wrecv.at[slot])
            pass_wave(slot, XUP, xup)
            pass_wave(slot, XDOWN, xdown)
            pass_mate(slot)
            slot = z * 8 + yy

            @pl.when(i > 0)
            def _():
                wait(env.at[slot], erecv.at[slot])

            pass_env(slot, ZUP, zup)
            pass_env(slot, ZDOWN, zdown)

        @pl.when(jnp.logical_and(i >= 1, i < 9))
        def _():
            yy = source(i - 1)
            even = yy % 2 == 0
            low = (2 * ((x + 3) % 4) + c) * 8 + yy
            wait(wave.at[low], wrecv.at[low])

            @pl.when(even)
            def _():
                pass_wave(low, XUP, xup)

            pass_mate(low)
            high = (2 * ((x + 1) % 4) + c) * 8 + yy
            wait(wave.at[high], wrecv.at[high])

            @pl.when(jnp.logical_not(even))
            def _():
                pass_wave(high, XDOWN, xdown)

            pass_mate(high)
            low, high = ((z + 7) % 8) * 8 + yy, ((z + 1) % 8) * 8 + yy
            wait(env.at[low], erecv.at[low])
            pass_env(low, ZUP, zup)
            wait(env.at[high], erecv.at[high])
            pass_env(high, ZDOWN, zdown)

        @pl.when(jnp.logical_and(i >= 2, i < 10))
        def _():
            yy = source(i - 2)
            far = (2 * ((x + 2) % 4) + c) * 8 + yy
            wait(wave.at[far], wrecv.at[far])
            pass_mate(far)
            low, high = ((z + 6) % 8) * 8 + yy, ((z + 2) % 8) * 8 + yy
            wait(env.at[low], erecv.at[low])
            pass_env(low, ZUP, zup)
            wait(env.at[high], erecv.at[high])
            pass_env(high, ZDOWN, zdown)

        @pl.when(jnp.logical_and(i >= 3, i < 11))
        def _():
            yy = source(i - 3)
            even = yy % 2 == 0
            low, high = ((z + 5) % 8) * 8 + yy, ((z + 3) % 8) * 8 + yy
            wait(env.at[low], erecv.at[low])

            @pl.when(even)
            def _():
                pass_env(low, ZUP, zup)

            wait(env.at[high], erecv.at[high])

            @pl.when(jnp.logical_not(even))
            def _():
                pass_env(high, ZDOWN, zdown)

        @pl.when(i >= 4)
        def _():
            far = ((z + 4) % 8) * 8 + source(i - 4)
            wait(env.at[far], erecv.at[far])

        return carry

    lax.fori_loop(0, 12, turn, 0)
    wait(rows, rows_recv)
    wait(wave.at[pl.ds(0, 32)], mate_recv)
    wait(wave.at[pl.ds(0, 7)], send.at[Y_SEND])
    wait(env.at[pl.ds(0, 7)], send.at[EY_SEND])
    wait(wave.at[pl.ds(0, 32)], send.at[MATE_SEND])
    wait(wave.at[pl.ds(0, 12)], send.at[XUP])
    wait(wave.at[pl.ds(0, 12)], send.at[XDOWN])
    wait(env.at[pl.ds(0, 28)], send.at[ZUP])
    wait(env.at[pl.ds(0, 28)], send.at[ZDOWN])

    @pl.when(jnp.logical_not(fixed))
    def _():
        wait(env.at[0], send.at[E_SEND])
        wait(rows, send.at[ROWS_SEND])


def gather(rows, left, right, outgoing):
    return pl.pallas_call(
        gather_kernel,
        out_shape=(
            jax.ShapeDtypeStruct((ROWS, 128), jnp.int32),
            jax.ShapeDtypeStruct((64, 2, 128, 128), jnp.bfloat16),
            jax.ShapeDtypeStruct((64, 4, 128, 128), jnp.bfloat16),
        ),
        in_specs=[ANY] * 4,
        out_specs=[ANY] * 3,
        scratch_shapes=[
            pltpu.SemaphoreType.DMA((64,)),
            pltpu.SemaphoreType.DMA((64,)),
            pltpu.SemaphoreType.DMA,
            pltpu.SemaphoreType.DMA,
            pltpu.SemaphoreType.DMA((9,)),
        ],
        compiler_params=pltpu.CompilerParams(collective_id=0, has_side_effects=True),
        name="gather",
    )(rows, left, right, outgoing)


def tasks_kernel(rows, env_any, wave_any, out_ref, env, wave, acc, inter, total, sems):
    loads = [
        pltpu.make_async_copy(wave_any, wave, sems.at[0]),
        pltpu.make_async_copy(env_any, env, sems.at[1]),
    ]
    for load in loads:
        load.start()
    acc[...] = jnp.zeros_like(acc)
    total[...] = jnp.zeros_like(total)
    for load in loads:
        load.wait()

    def left_step(t, carry):
        e, s, x = rows[3 * t], rows[3 * t + 1], rows[3 * t + 2]
        rhs = jnp.concatenate([wave[2 * s], wave[2 * s + 1]], axis=1)
        acc[x] += jnp.dot(env[e, 0], rhs, preferred_element_type=jnp.float32)
        return carry

    lax.fori_loop(0, LEFT, left_step, 0, unroll=4)
    for v in range(2):
        inter[:, v] = acc[:, :, 128 * v : 128 * (v + 1)].astype(jnp.bfloat16)

    def right_step(t, carry):
        base = 3 * (LEFT + t)
        x, e, k = rows[base], rows[base + 1], rows[base + 2]
        lhs = inter[x].reshape(256, 128)
        total[k] += jnp.dot(lhs, env[e, 1], preferred_element_type=jnp.float32)
        return carry

    lax.fori_loop(0, RIGHT, right_step, 0, unroll=4)
    for k in range(TILES):
        out_ref[:, k] = jnp.swapaxes(total[k].reshape(2, 8, 16, 128), 0, 1).astype(jnp.bfloat16)


def run_tasks(rows, env, wave):
    return pl.pallas_call(
        tasks_kernel,
        out_shape=jax.ShapeDtypeStruct((8, TILES, 2, 16, 128), jnp.bfloat16),
        in_specs=[SMEM, ANY, ANY],
        out_specs=VMEM,
        scratch_shapes=[
            pltpu.VMEM((64, 2, 128, 128), jnp.bfloat16),
            pltpu.VMEM((256, 128, 128), jnp.bfloat16),
            pltpu.VMEM((INTER_TILES, 128, 256), jnp.float32),
            pltpu.VMEM((INTER_TILES, 2, 128, 128), jnp.bfloat16),
            pltpu.VMEM((TILES, 256, 128), jnp.float32),
            pltpu.SemaphoreType.DMA((2,)),
        ],
        compiler_params=pltpu.CompilerParams(vmem_limit_bytes=44 << 20),
        name="tasks",
    )(rows, env, wave)


def reduce_kernel(partial, out, parts, result, arrived, recv, send, last_recv, last_send):
    z, x, y, c = place()
    xc = 2 * x + c
    fixed = z == xc
    partner = swapped(z, x, y, c)
    peers = []
    for k in range(1, 8):
        to = (xc + k) % 8
        peers.append((z, to // 2, y, to % 2))
    greet(peers, partner, fixed)
    copies = []
    for k in (1, 7, 2, 6, 3, 5, 4):
        copy = pltpu.make_async_remote_copy(
            src_ref=partial.at[(xc + k) % 8], dst_ref=parts.at[k],
            send_sem=send.at[k], recv_sem=recv.at[k],
            device_id=peers[k - 1], device_id_type=MESH,
        )
        copy.start()
        copies.append(copy)
    for copy in copies:
        copy.wait_recv()
    for h in range(2):
        rows = pl.ds(256 * h, 256)
        total = partial[xc, rows].astype(jnp.float32)
        for k in range(1, 8):
            total += parts[k, rows].astype(jnp.float32)
        result[rows] = total.astype(jnp.bfloat16)

        @pl.when(fixed)
        def _():
            pltpu.make_async_copy(result.at[rows], arrived.at[rows], last_recv.at[h]).start()

        @pl.when(jnp.logical_not(fixed))
        def _():
            pltpu.make_async_remote_copy(
                src_ref=result.at[rows], dst_ref=arrived.at[rows],
                send_sem=last_send.at[h], recv_sem=last_recv.at[h],
                device_id=partner, device_id_type=MESH,
            ).start()

    for copy in copies:
        copy.wait_send()
    for h in range(2):
        rows = pl.ds(256 * h, 256)
        pltpu.make_async_copy(result.at[rows], arrived.at[rows], last_recv.at[h]).wait()
        out[rows] = arrived[rows].astype(jnp.float32)

        @pl.when(jnp.logical_not(fixed))
        def _():
            pltpu.make_async_copy(result.at[rows], arrived.at[rows], last_send.at[h]).wait()


def reduce(partial):
    return pl.pallas_call(
        reduce_kernel,
        out_shape=jax.ShapeDtypeStruct((512, 128), jnp.float32),
        in_specs=[VMEM],
        out_specs=VMEM,
        scratch_shapes=[
            pltpu.VMEM((8, 512, 128), jnp.bfloat16),
            pltpu.VMEM((512, 128), jnp.bfloat16),
            pltpu.VMEM((512, 128), jnp.bfloat16),
            pltpu.SemaphoreType.DMA((8,)),
            pltpu.SemaphoreType.DMA((8,)),
            pltpu.SemaphoreType.DMA((2,)),
            pltpu.SemaphoreType.DMA((2,)),
        ],
        compiler_params=pltpu.CompilerParams(collective_id=1, has_side_effects=True),
        name="reduce",
    )(partial)


def shards(wave_tiles, left_env, right_env, send_list, left_tasks, right_tasks):
    z = lax.axis_index("z")
    left_rows, right_rows = left_tasks[0, 0], right_tasks[0, 0]
    env_place = lambda e: ((e >> 4) << 4) | ((e & 1) << 3) | ((e >> 1) & 7)
    slot = left_rows[:, 1]
    sender = slot >> 1
    spot = ((((sender >> 4) << 1) | (sender & 1)) << 4) | (((sender >> 1) & 7) << 1) | (slot & 1)
    left_rows = jnp.stack([env_place(left_rows[:, 0]), spot, left_rows[:, 2]], axis=1)
    right_rows = jnp.stack(
        [right_rows[:, 0], env_place(right_rows[:, 1]), right_rows[:, 2]], axis=1
    )
    rows = jnp.concatenate([left_rows, right_rows], axis=0).reshape(-1)
    rows = jnp.pad(rows, (0, ROWS * 128 - rows.shape[0])).reshape(ROWS, 128)

    chosen = lax.dynamic_index_in_dim(send_list.reshape(4, 8, 2, 2), z // 2, 0, False)
    chosen = lax.dynamic_index_in_dim(chosen, z % 2, 1, False).reshape(16)
    picked = jnp.take(wave_tiles, jnp.maximum(chosen, 0), axis=0)
    outgoing = jnp.where((chosen >= 0)[:, None, None, None], picked, jnp.zeros((), jnp.bfloat16))

    rows, env, wave = gather(rows, left_env[0, 0], right_env[0, 0], outgoing.reshape(8, 4, 128, 128))
    partial = run_tasks(rows.reshape(-1), env, wave.reshape(256, 128, 128))
    return reduce(partial.reshape(8, 512, 128)).reshape(TILES, 2, 16, 128)


def solution(mesh):
    fine = Mesh(mesh.devices.reshape(8, 4, 8, 2), AXES)
    sector = ("x", "y", "core")
    in_specs = (
        P(sector, None, None, None),
        P("z", sector, None, None),
        P("z", sector, None, None),
        P(sector, None),
        P("z", sector, None, None),
        P("z", sector, None, None),
    )
    out_specs = P(sector, None, "z", None)
    return jax.shard_map(shards, mesh=fine, in_specs=in_specs, out_specs=out_specs, check_vma=False)
```

time: 347 us -> 150 us (0.43)
  waiting for transfers between devices: 239 us -> 0 us
  Pallas kernels: 26 us -> 136 us
  blocking collectives: 36.9 us -> 0 us
  starting transfers between devices: 22.7 us -> 0 us
  between operations: 13.3 us -> 0.09 us
    all_gather x3 -> x0, waiting for transfers between devices: 172 us -> none  [the longest x1 83.6 us: shards(): left = lax.all_gather(env[0], ('y', 'z'), axis=0)]
    pallas_call x0 -> x2, Pallas kernels: none -> 112 us  [the longest x1 77.9 us: gather(): pl.pallas_call(gather_kernel, out_shape=(jax.ShapeDtypeStruct((ROWS, 128)...]
    reduce_scatter x1 -> x0, waiting for transfers between devices: 40.1 us -> none  [shards(): lax.psum_scatter(partial, ('x', 'core'), scatter_dimension=0, tiled=False)]
    all_to_all x1 -> x0, blocking collectives: 36.9 us -> none  [shards(): lax.all_to_all(outgoing, 'y', split_axis=0, concat_axis=0, tiled=True)]
    ppermute x3 -> x0, waiting for transfers between devices: 26 us -> none  [the longest x1 17.9 us: shards(): return lax.ppermute(summed, AXES, SWAP)]
    ppermute x3 -> x0, starting transfers between devices: 22.6 us -> none  [the longest x1 11.1 us: shards(): env = lax.ppermute(env, AXES, SWAP)]
    unnamed x14 -> x13, local copies, waits for them, and re-layouts: 4.44 us -> 7.48 us
  transfers between devices with their start and end apart: 7 -> 0, of which waited for: 7 -> 0; matrix products, arithmetic and copies ran while one was open for 1% -> 0% of each run, Pallas kernels for 0% -> 0%
where the time goes in v2:
time: 150 us; the launch traced here: 149 us
  Pallas kernels  136 us (91%)
  local copies, waits for them, and re-layouts  9.77 us (7%)
  other arithmetic  2.67 us (2%)
    pallas_call x1, Pallas kernels, gather(): pl.pallas_call(gather_kernel, out_shape=(jax.ShapeDtypeStruct((ROWS, 128)...  77.9 us
    pallas_call x1, Pallas kernels, reduce(): pl.pallas_call(reduce_kernel, out_shape=jax.ShapeDtypeStruct((512, 128),...  33.7 us
    pallas_call x1, Pallas kernels, run_tasks(): pl.pallas_call(tasks_kernel, out_shape=jax.ShapeDtypeStruct((8, TILES, 2,...  24.6 us
    unnamed x13, local copies, waits for them, and re-layouts  7.48 us

profile of v2, /device:TPU:7, one launch (start us, length us, event | category | flops | bytes accessed | tf_op | source)
XLA Modules:
  0.0 148.7 jit_solution(4855725920453979456)
XLA Ops:
  0.0 0.5 broadcast.114
  0.5 1.3 reduce.4
  1.8 0.7 copy.27
  2.5 0.7 copy.26
  3.2 0.1 add_add_fusion
  3.3 0.2 reshape.66
  3.5 0.1 copy.23
  3.6 0.1 copy.18
  3.7 0.1 copy.19
  3.8 0.1 copy.20
  3.9 0.1 reshape.73
  4.0 0.1 copy.16
  4.2 0.2 reshape.64
  4.4 0.6 pad_bitcast_fusion.rows_in
  5.0 0.7 gather_fusion
  5.7 1.2 fusion.outgoing
  7.0 77.9 %gather.11 = (s32[16,128]{1,0:T(8,128)}, bf16[64,2,128,128]{3,2,1,0:T(8,128)(2,1)}, bf16[64,4,128,128]{3,2,1,0:T(8,128)(2,1)}) custom-call(s32[16,128]{1,0:T(8,128)} %pad_bitcast_fusion.rows_in, bf16[128,128]{1,0:T(8,128)(2,1)} %bitcast.36, bf16[128,128]{1,0:T(8,128)(2,1)} %bitcast.37, bf16[8,4,128,128]{3,2,1,0:T(8,128)(2,1)} %fusion.outgoing), custom_call_target="tpu_custom_call" | custom-call | tf_op jit(solution)/shard_map/gather/pallas_call | solution.py:201
  84.9 0.0 copy-start.1
  84.9 2.2 %copy-done.1 = bf16[64,2,128,128]{3,2,1,0:T(8,128)(2,1)S(1)} copy-done((bf16[64,2,128,128]{3,2,1,0:T(8,128)(2,1)S(1)}, bf16[64,2,128,128]{3,2,1,0:T(8,128)(2,1)}, u32[]{:S(2)}) %copy-start.1) | copy-done | bytes 4194328
  87.1 0.7 copy-done.3
  87.7 24.6 %tasks.1 = bf16[8,16,2,16,128]{4,3,2,1,0:T(8,128)(2,1)S(1)} custom-call(s32[2048]{0:T(1024)S(1)} %bitcast.32, bf16[64,2,128,128]{3,2,1,0:T(8,128)(2,1)S(1)} %copy-done.1, bf16[256,128,128]{2,1,0:T(8,128)(2,1)} %bitcast.33), custom_call_target="tpu_custom_call" | custom-call | tf_op jit(solution)/shard_map/tasks/pallas_call | solution.py:257
  112.4 1.0 copy-done.2
  113.3 33.7 %reduce.5 = f32[512,128]{1,0:T(8,128)} custom-call(bf16[8,512,128]{2,1,0:T(8,128)(2,1)} %bitcast.31), custom_call_target="tpu_custom_call" | custom-call | tf_op jit(solution)/shard_map/reduce/pallas_call | solution.py:328
  147.0 1.7 %copy.29 = f32[16,2,16,128]{3,2,1,0:T(8,128)} copy(f32[16,2,16,128]{3,2,1,0:T(8,128)} %bitcast.35) | data formatting | bytes 524288
  (14 shorter events, 0.1 us)
Async XLA Ops:
  0.0 5.0 %copy-start = (bf16[16,2,128,128]{3,2,1,0:T(8,128)(2,1)S(1)}, bf16[16,2,128,128]{3,2,1,0:T(8,128)(2,1)}, u32[]{:S(2)}) copy-start(bf16[16,2,128,128]{3,2,1,0:T(8,128)(2,1)} %param.6) | copy-start | bytes 3145732
  84.9 2.2 %copy-start.1 = (bf16[64,2,128,128]{3,2,1,0:T(8,128)(2,1)S(1)}, bf16[64,2,128,128]{3,2,1,0:T(8,128)(2,1)}, u32[]{:S(2)}) copy-start(bf16[64,2,128,128]{3,2,1,0:T(8,128)(2,1)} %get-tuple-element.9.env_any) | copy-start | bytes 12582916
  87.1 0.7 copy-start.3
  112.3 1.0 copy-start.2

commit v3 on v0

v3 whole, which is shorter than its diff:
```python
import jax
import jax.numpy as jnp
from jax import lax
from jax.experimental import pallas as pl
from jax.experimental.pallas import tpu as pltpu
from jax.sharding import Mesh
from jax.sharding import PartitionSpec as P

TILES = 16
LEFT_PAIRS = 64
RIGHT_PAIRS = 136
AXES = ("z", "x", "y", "core")
MESH = pl.DeviceIdType.MESH
ANY = pl.BlockSpec(memory_space=pl.ANY)
VMEM = pl.BlockSpec(memory_space=pltpu.VMEM)
SMEM = pl.BlockSpec(memory_space=pltpu.SMEM)


def place():
    return tuple(lax.axis_index(name) for name in AXES)


def swapped(z, x, y, c):
    return (2 * x + c, z // 2, y, z % 2)


def prep_kernel(wave, picks, left, right, outgoing, lists):
    z = lax.axis_index("z")
    for to in range(8):
        owner = (z // 2 * 8 + to) * 2 + z % 2
        for slot in range(2):
            index = picks[0, 2 * owner + slot]
            tile = wave[jnp.maximum(index, 0)]
            outgoing[2 * to + slot] = jnp.where(index >= 0, tile, jnp.zeros_like(tile))

    def iota(shape, axis):
        return lax.broadcasted_iota(jnp.int32, shape, axis)

    def total(mask, value, axis):
        return jnp.sum(jnp.where(mask, value, 0), axis=axis, keepdims=True)

    def column(row):
        n = row.shape[1]
        return total(iota((n, n), 0) == iota((n, n), 1), row, 1)

    def ordered(row):
        n = row.shape[1]
        down, across = iota((n, n), 0), iota((n, n), 1)
        key = column(row)
        same = key == row
        within = total(jnp.logical_and(same, across < down), 1, 1)
        later = total(jnp.logical_and(same, across > down), 1, 1)
        within_row = total(jnp.logical_and(same, down < across), 1, 0)
        start = total(row < key, 1 - (within_row & 1), 1)
        return key, within, 2 * start + within, later == 0

    def env_place(e):
        return ((e >> 4) << 4) | ((e & 1) << 3) | ((e >> 1) & 7)

    key, within, spot, last = ordered(left[2:3])
    slot = left[1:2]
    sender = slot >> 1
    source = ((((sender >> 4) << 1) | (sender & 1)) << 4) | (((sender >> 1) & 7) << 1) | (slot & 1)
    value = column(env_place(left[0:1]) * 256 + source) + jnp.where(within > 0, 65536, 0)
    n = left.shape[1]
    lists[0:1] = 128 + total(spot == iota((n, 128), 1), value - 128, 0)
    n_right = right.shape[1]
    hit = jnp.logical_and(key == right[0:1], last)
    made = LEFT_PAIRS + total(hit, (spot >> 1) - LEFT_PAIRS, 0)
    key, within, spot, last = ordered(right[2:3])
    value = column(made * 256 + env_place(right[1:2])) + jnp.where(within > 0, 65536, 0)
    empty = LEFT_PAIRS * 256
    for part in range(3):
        place = iota((n_right, 128), 1) + 128 * part
        lists[1 + part : 2 + part] = empty + total(spot == place, value - empty, 0)
    hit = jnp.logical_and(key == iota((n_right, 128), 1), last)
    lists[4:5] = RIGHT_PAIRS + total(hit, (spot >> 1) - RIGHT_PAIRS, 0)
    lists[5:8] = jnp.zeros((3, 128), jnp.int32)


def prep(wave, picks, left, right):
    return pl.pallas_call(
        prep_kernel,
        out_shape=(
            jax.ShapeDtypeStruct((16, 2, 128, 128), jnp.bfloat16),
            jax.ShapeDtypeStruct((8, 128), jnp.int32),
        ),
        in_specs=[VMEM, SMEM, VMEM, VMEM],
        out_specs=(VMEM, VMEM),
        name="prep",
    )(wave, picks, left, right)


def main_kernel(
    lists_in, left_in, right_in, outgoing, out,
    lists_vmem, lists, wave, env, inter, cumulated, partial, parts, result,
    wrecv, erecv, mate_recv, lists_recv, send, recv, part_send, last_recv, last_send,
):
    z, x, y, c = place()
    xc = 2 * x + c
    fixed = z == xc
    partner = swapped(z, x, y, c)
    mate = (z, x, y, 1 - c)
    xup, xdown = (z, (x + 1) % 4, y, c), (z, (x + 3) % 4, y, c)
    zup, zdown = ((z + 1) % 8, x, y, c), ((z + 7) % 8, x, y, c)
    peers = [(z, (xc + k) % 8 // 2, y, (xc + k) % 8 % 2) for k in range(1, 8)]

    barrier = pltpu.get_barrier_semaphore()
    for peer in peers + [zup, zdown] + [(z, x, (y + d) % 8, c) for d in range(1, 8)]:
        pl.semaphore_signal(barrier, inc=1, device_id=peer, device_id_type=MESH)

    @pl.when(jnp.logical_not(fixed))
    def _():
        pl.semaphore_signal(barrier, inc=1, device_id=partner, device_id_type=MESH)

    wave[128] = jnp.zeros((2, 128, 128), jnp.bfloat16)
    inter[LEFT_PAIRS] = jnp.zeros((2, 128, 128), jnp.bfloat16)
    cumulated[RIGHT_PAIRS] = jnp.zeros((256, 128), jnp.bfloat16)
    pl.semaphore_wait(barrier, 16 + jnp.where(fixed, 0, 1))
    Y_SEND, EY_SEND, MATE_SEND, XUP, XDOWN, ZUP, ZDOWN, E_SEND, LISTS_SEND = range(9)

    def remote(source, target, sender, receiver, device):
        pltpu.make_async_remote_copy(
            src_ref=source, dst_ref=target, send_sem=send.at[sender], recv_sem=receiver,
            device_id=device, device_id_type=MESH,
        ).start()

    def wait(ref, sem):
        pltpu.make_async_copy(ref, ref, sem).wait()

    def chunks(slot, count=1):
        return wave.at[pl.ds(2 * slot, 2 * count)]

    def pass_wave(slot, sender, device):
        remote(chunks(slot), chunks(slot), sender, wrecv.at[slot], device)

    def pass_mate(slot):
        remote(chunks(slot), chunks(slot), MATE_SEND, mate_recv, mate)

    def pass_env(slot, sender, device):
        remote(env.at[slot], env.at[slot], sender, erecv.at[slot], device)

    mine = xc * 8 + y

    @pl.when(fixed)
    def _():
        pltpu.make_async_copy(left_in, env.at[mine, 0], erecv.at[mine]).start()
        pltpu.make_async_copy(right_in, env.at[mine, 1], erecv.at[mine]).start()
        pltpu.make_async_copy(lists_in, lists_vmem, lists_recv).start()

    @pl.when(jnp.logical_not(fixed))
    def _():
        remote(left_in, env.at[mine, 0], E_SEND, erecv.at[mine], partner)
        remote(right_in, env.at[mine, 1], E_SEND, erecv.at[mine], partner)
        remote(lists_in, lists_vmem, LISTS_SEND, lists_recv, partner)

    own = z * 8 + y

    def shift(r):
        step = (r + 1) // 2
        return jnp.where(r % 2 == 1, step, 8 - step)

    def send_wave(r):
        to = (y + 8 - shift(r)) % 8
        remote(outgoing.at[pl.ds(2 * to, 2)], chunks(mine), Y_SEND, wrecv.at[mine], (z, x, to, c))

    def send_env(r):
        to = (y + 8 - shift(r)) % 8
        remote(env.at[own], env.at[own], EY_SEND, erecv.at[own], (z, x, to, c))

    here = outgoing.at[pl.ds(2 * y, 2)]
    pltpu.make_async_copy(here, chunks(mine), wrecv.at[mine]).start()
    for r in range(1, 5):
        send_wave(r)
    remote(here, chunks(mine), XUP, wrecv.at[mine], xup)
    remote(here, chunks(mine), XDOWN, wrecv.at[mine], xdown)
    remote(here, chunks(mine), MATE_SEND, mate_recv, mate)
    wait(env.at[own], erecv.at[own])
    for r in range(1, 5):
        send_env(r)

    def source(r):
        return (y + shift(r)) % 8

    def turn(i, carry):
        @pl.when(i < 3)
        def _():
            send_env(i + 5)
            send_wave(i + 5)

        @pl.when(i < 8)
        def _():
            yy = source(i)
            slot = xc * 8 + yy

            @pl.when(i > 0)
            def _():
                wait(chunks(slot), wrecv.at[slot])
                pass_wave(slot, XUP, xup)
                pass_wave(slot, XDOWN, xdown)
                pass_mate(slot)

            slot = z * 8 + yy

            @pl.when(i > 0)
            def _():
                wait(env.at[slot], erecv.at[slot])

            pass_env(slot, ZUP, zup)
            pass_env(slot, ZDOWN, zdown)

        @pl.when(jnp.logical_and(i >= 1, i < 9))
        def _():
            yy = source(i - 1)
            even = yy % 2 == 0
            low = (2 * ((x + 3) % 4) + c) * 8 + yy
            wait(chunks(low), wrecv.at[low])

            @pl.when(even)
            def _():
                pass_wave(low, XUP, xup)

            pass_mate(low)
            high = (2 * ((x + 1) % 4) + c) * 8 + yy
            wait(chunks(high), wrecv.at[high])

            @pl.when(jnp.logical_not(even))
            def _():
                pass_wave(high, XDOWN, xdown)

            pass_mate(high)
            low, high = ((z + 7) % 8) * 8 + yy, ((z + 1) % 8) * 8 + yy
            wait(env.at[low], erecv.at[low])
            pass_env(low, ZUP, zup)
            wait(env.at[high], erecv.at[high])
            pass_env(high, ZDOWN, zdown)

        @pl.when(jnp.logical_and(i >= 2, i < 10))
        def _():
            yy = source(i - 2)
            far = (2 * ((x + 2) % 4) + c) * 8 + yy
            wait(chunks(far), wrecv.at[far])
            pass_mate(far)
            low, high = ((z + 6) % 8) * 8 + yy, ((z + 2) % 8) * 8 + yy
            wait(env.at[low], erecv.at[low])
            pass_env(low, ZUP, zup)
            wait(env.at[high], erecv.at[high])
            pass_env(high, ZDOWN, zdown)

        @pl.when(jnp.logical_and(i >= 3, i < 11))
        def _():
            yy = source(i - 3)
            even = yy % 2 == 0
            low, high = ((z + 5) % 8) * 8 + yy, ((z + 3) % 8) * 8 + yy
            wait(env.at[low], erecv.at[low])

            @pl.when(even)
            def _():
                pass_env(low, ZUP, zup)

            wait(env.at[high], erecv.at[high])

            @pl.when(jnp.logical_not(even))
            def _():
                pass_env(high, ZDOWN, zdown)

        @pl.when(i >= 4)
        def _():
            far = ((z + 4) % 8) * 8 + source(i - 4)
            wait(env.at[far], erecv.at[far])

        return carry

    lax.fori_loop(0, 12, turn, 0)

    wait(lists_vmem, lists_recv)
    load = pltpu.make_async_copy(lists_vmem, lists, lists_recv)
    load.start()
    wait(chunks(mine), wrecv.at[mine])
    wait(chunks(0, 32), mate_recv)
    load.wait()

    def left_pair(p, total):
        one, two = lists[0, 2 * p], lists[0, 2 * p + 1]
        lhs = jnp.concatenate([env[(one >> 8) & 63, 0], env[(two >> 8) & 63, 0]], axis=1)
        rhs = jnp.concatenate(
            [
                jnp.concatenate([wave[one & 255, 0], wave[one & 255, 1]], axis=1),
                jnp.concatenate([wave[two & 255, 0], wave[two & 255, 1]], axis=1),
            ],
            axis=0,
        )
        product = jnp.dot(lhs, rhs, preferred_element_type=jnp.float32)
        total = product + total * (one >> 16).astype(jnp.float32)
        inter[p, 0] = total[:, :128].astype(jnp.bfloat16)
        inter[p, 1] = total[:, 128:].astype(jnp.bfloat16)
        return total

    lax.fori_loop(0, LEFT_PAIRS, left_pair, jnp.zeros((128, 256), jnp.float32), unroll=8)

    def right_pair(p, total):
        row, column = 1 + p // 64, 2 * (p % 64)
        one, two = lists[row, column], lists[row, column + 1]
        lhs = jnp.concatenate(
            [
                inter[(one >> 8) & 127].reshape(256, 128),
                inter[(two >> 8) & 127].reshape(256, 128),
            ],
            axis=1,
        )
        rhs = jnp.concatenate([env[one & 63, 1], env[two & 63, 1]], axis=0)
        product = jnp.dot(lhs, rhs, preferred_element_type=jnp.float32)
        total = product + total * (one >> 16).astype(jnp.float32)
        cumulated[p] = total.astype(jnp.bfloat16)
        return total

    lax.fori_loop(0, RIGHT_PAIRS, right_pair, jnp.zeros((256, 128), jnp.float32), unroll=8)
    for k in range(TILES):
        tile = cumulated[lists[4, k]].reshape(2, 8, 16, 128)
        partial[:, k] = jnp.swapaxes(tile, 0, 1)

    def part(k):
        return pltpu.make_async_remote_copy(
            src_ref=partial.at[(xc + k) % 8], dst_ref=parts.at[k],
            send_sem=part_send.at[k], recv_sem=recv.at[k],
            device_id=peers[k - 1], device_id_type=MESH,
        )

    copies = [part(k) for k in (1, 7, 2, 6, 3, 5, 4)]
    for copy in copies:
        copy.start()
    for copy in copies:
        copy.wait_recv()
    for h in range(2):
        half = pl.ds(8 * h, 8)
        total = partial[xc, half].astype(jnp.float32)
        for k in range(1, 8):
            total += parts[k, half].astype(jnp.float32)
        result[half] = total.astype(jnp.bfloat16)

        @pl.when(fixed)
        def _():
            pltpu.make_async_copy(result.at[half], out.at[half], last_recv.at[h]).start()

        @pl.when(jnp.logical_not(fixed))
        def _():
            pltpu.make_async_remote_copy(
                src_ref=result.at[half], dst_ref=out.at[half],
                send_sem=last_send.at[h], recv_sem=last_recv.at[h],
                device_id=partner, device_id_type=MESH,
            ).start()

    wait(chunks(0, 7), send.at[Y_SEND])
    wait(env.at[pl.ds(0, 7)], send.at[EY_SEND])
    wait(chunks(0, 32), send.at[MATE_SEND])
    wait(chunks(0, 12), send.at[XUP])
    wait(chunks(0, 12), send.at[XDOWN])
    wait(env.at[pl.ds(0, 28)], send.at[ZUP])
    wait(env.at[pl.ds(0, 28)], send.at[ZDOWN])
    for copy in copies:
        copy.wait_send()

    @pl.when(jnp.logical_not(fixed))
    def _():
        wait(env.at[0], send.at[E_SEND])
        wait(lists_vmem, send.at[LISTS_SEND])
        for h in range(2):
            wait(result.at[pl.ds(8 * h, 8)], last_send.at[h])

    for h in range(2):
        wait(result.at[pl.ds(8 * h, 8)], last_recv.at[h])


def main(lists, left, right, outgoing):
    return pl.pallas_call(
        main_kernel,
        out_shape=jax.ShapeDtypeStruct((TILES, 2, 16, 128), jnp.bfloat16),
        in_specs=[VMEM, ANY, ANY, VMEM],
        out_specs=VMEM,
        scratch_shapes=[
            pltpu.VMEM((8, 128), jnp.int32),
            pltpu.SMEM((8, 128), jnp.int32),
            pltpu.VMEM((129, 2, 128, 128), jnp.bfloat16),
            pltpu.VMEM((64, 2, 128, 128), jnp.bfloat16),
            pltpu.VMEM((LEFT_PAIRS + 1, 2, 128, 128), jnp.bfloat16),
            pltpu.VMEM((RIGHT_PAIRS + 1, 256, 128), jnp.bfloat16),
            pltpu.VMEM((8, TILES, 2, 16, 128), jnp.bfloat16),
            pltpu.VMEM((8, TILES, 2, 16, 128), jnp.bfloat16),
            pltpu.VMEM((TILES, 2, 16, 128), jnp.bfloat16),
            pltpu.SemaphoreType.DMA((64,)),
            pltpu.SemaphoreType.DMA((64,)),
            pltpu.SemaphoreType.DMA,
            pltpu.SemaphoreType.DMA,
            pltpu.SemaphoreType.DMA((9,)),
            pltpu.SemaphoreType.DMA((8,)),
            pltpu.SemaphoreType.DMA((8,)),
            pltpu.SemaphoreType.DMA((2,)),
            pltpu.SemaphoreType.DMA((2,)),
        ],
        compiler_params=pltpu.CompilerParams(
            collective_id=0, has_side_effects=True, vmem_limit_bytes=44 << 20
        ),
        name="main",
    )(lists, left, right, outgoing)


def shards(wave_tiles, left_env, right_env, send_list, left_tasks, right_tasks):
    outgoing, lists = prep(wave_tiles, send_list, left_tasks[0, 0].T, right_tasks[0, 0].T)
    rows = main(lists, left_env[0, 0], right_env[0, 0], outgoing)
    return rows.astype(jnp.float32)


def solution(mesh):
    fine = Mesh(mesh.devices.reshape(8, 4, 8, 2), AXES)
    sector = ("x", "y", "core")
    in_specs = (
        P(sector, None, None, None),
        P("z", sector, None, None),
        P("z", sector, None, None),
        P(sector, None),
        P("z", sector, None, None),
        P("z", sector, None, None),
    )
    out_specs = P(sector, None, "z", None)
    return jax.shard_map(shards, mesh=fine, in_specs=in_specs, out_specs=out_specs, check_vma=False)
```

time: 565 us -> 114 us (0.20)
  the two profiles are of different devices: /device:TPU:7 before, /device:TPU:10 now
where the time goes in v3:
time: 114 us
  Pallas kernels  110 us (96%)
  local copies, waits for them, and re-layouts  3.87 us (3%)
    pallas_call x1, Pallas kernels, main(): pl.pallas_call(main_kernel, out_shape=jax.ShapeDtypeStruct((TILES, 2, 16,...  106 us
    unnamed x14, local copies, waits for them, and re-layouts  3.87 us
    pallas_call x1, Pallas kernels, prep(): pl.pallas_call(prep_kernel, out_shape=(jax.ShapeDtypeStruct((16, 2, 128,...  3.09 us

profile of v3, /device:TPU:10, one launch (start us, length us, event | category | flops | bytes accessed | tf_op | source)
XLA Modules:
  0.0 114.2 jit_solution(1552878649524464786)
XLA Ops:
  0.0 0.0 copy-start.5
  0.0 0.7 copy-done.5
  0.7 0.0 copy-start.4
  0.7 0.6 copy.12
  1.3 0.1 copy-done.4
  1.4 0.6 copy.11
  2.0 0.0 copy-start.1
  2.0 0.0 copy-start.2
  2.0 3.1 %prep.1 = (bf16[16,2,128,128]{3,2,1,0:T(8,128)(2,1)}, s32[8,128]{1,0:T(8,128)}) custom-call(bf16[16,2,128,128]{3,2,1,0:T(8,128)(2,1)} %wave.1, s32[1,128]{1,0:T(1,128)} %picks.1, s32[3,96]{1,0:T(4,128)} %bitcast.15, s32[3,256]{1,0:T(4,128)} %bitcast.14), custom_call_target="tpu_custom_call" | custom-call | tf_op jit(solution)/shard_map/prep/pallas_call | solution.py:82
  5.1 0.0 copy-done.1
  5.1 0.0 copy-done.2
  5.1 0.0 copy-start
  5.1 1.2 %copy-done = bf16[16,2,128,128]{3,2,1,0:T(8,128)(2,1)S(1)} copy-done((bf16[16,2,128,128]{3,2,1,0:T(8,128)(2,1)S(1)}, bf16[16,2,128,128]{3,2,1,0:T(8,128)(2,1)}, u32[]{:S(2)}) %copy-start) | copy-done | bytes 1048600
  6.3 0.0 copy-start.3
  6.3 0.7 copy-done.3
  7.0 106.5 %main.1 = bf16[16,2,16,128]{3,2,1,0:T(8,128)(2,1)S(1)} custom-call(s32[8,128]{1,0:T(8,128)S(1)} %copy-done.3, bf16[128,128]{1,0:T(8,128)(2,1)S(1)} %bitcast.12, bf16[128,128]{1,0:T(8,128)(2,1)S(1)} %bitcast.13, bf16[16,2,128,128]{3,2,1,0:T(8,128)(2,1)S(1)} %copy-done), custom_call_target="tpu_custom_call" | custom-call | tf_op jit(solution)/shard_map/main/pallas_call | solution.py:375
  113.5 0.7 convert_element_type.3
Async XLA Ops:
  0.0 0.7 copy-start.5
  0.7 0.7 copy-start.4
  2.0 3.1 %copy-start.1 = (bf16[1,1,128,128]{3,2,1,0:T(8,128)(2,1)S(1)}, bf16[1,1,128,128]{3,2,1,0:T(8,128)(2,1)}, u32[]{:S(2)}) copy-start(bf16[1,1,128,128]{3,2,1,0:T(8,128)(2,1)} %param.7) | copy-start | bytes 98308
  2.0 3.1 %copy-start.2 = (bf16[1,1,128,128]{3,2,1,0:T(8,128)(2,1)S(1)}, bf16[1,1,128,128]{3,2,1,0:T(8,128)(2,1)}, u32[]{:S(2)}) copy-start(bf16[1,1,128,128]{3,2,1,0:T(8,128)(2,1)} %param.8) | copy-start | bytes 98308
  5.1 1.2 %copy-start = (bf16[16,2,128,128]{3,2,1,0:T(8,128)(2,1)S(1)}, bf16[16,2,128,128]{3,2,1,0:T(8,128)(2,1)}, u32[]{:S(2)}) copy-start(bf16[16,2,128,128]{3,2,1,0:T(8,128)(2,1)} %get-tuple-element.8.outgoing) | copy-start | bytes 3145732
  6.3 0.7 copy-start.3

commit v4 on v3

--- a/solution.py
+++ b/solution.py
@@ -9,6 +9,7 @@
 TILES = 16
 LEFT_PAIRS = 64
 RIGHT_PAIRS = 136
+STEPS = 4
 AXES = ("z", "x", "y", "core")
 MESH = pl.DeviceIdType.MESH
 ANY = pl.BlockSpec(memory_space=pl.ANY)
@@ -24,15 +25,7 @@
     return (2 * x + c, z // 2, y, z % 2)
 
 
-def prep_kernel(wave, picks, left, right, outgoing, lists):
-    z = lax.axis_index("z")
-    for to in range(8):
-        owner = (z // 2 * 8 + to) * 2 + z % 2
-        for slot in range(2):
-            index = picks[0, 2 * owner + slot]
-            tile = wave[jnp.maximum(index, 0)]
-            outgoing[2 * to + slot] = jnp.where(index >= 0, tile, jnp.zeros_like(tile))
-
+def build_lists(left, right, lists):
     def iota(shape, axis):
         return lax.broadcasted_iota(jnp.int32, shape, axis)
 
@@ -57,18 +50,18 @@
     def env_place(e):
         return ((e >> 4) << 4) | ((e & 1) << 3) | ((e >> 1) & 7)
 
-    key, within, spot, last = ordered(left[2:3])
-    slot = left[1:2]
+    key, within, spot, last = ordered(left[2])
+    slot = left[1]
     sender = slot >> 1
     source = ((((sender >> 4) << 1) | (sender & 1)) << 4) | (((sender >> 1) & 7) << 1) | (slot & 1)
-    value = column(env_place(left[0:1]) * 256 + source) + jnp.where(within > 0, 65536, 0)
-    n = left.shape[1]
+    value = column(env_place(left[0]) * 256 + source) + jnp.where(within > 0, 65536, 0)
+    n = left.shape[2]
     lists[0:1] = 128 + total(spot == iota((n, 128), 1), value - 128, 0)
-    n_right = right.shape[1]
-    hit = jnp.logical_and(key == right[0:1], last)
+    n_right = right.shape[2]
+    hit = jnp.logical_and(key == right[0], last)
     made = LEFT_PAIRS + total(hit, (spot >> 1) - LEFT_PAIRS, 0)
-    key, within, spot, last = ordered(right[2:3])
-    value = column(made * 256 + env_place(right[1:2])) + jnp.where(within > 0, 65536, 0)
+    key, within, spot, last = ordered(right[2])
+    value = column(made * 256 + env_place(right[1])) + jnp.where(within > 0, 65536, 0)
     empty = LEFT_PAIRS * 256
     for part in range(3):
         place = iota((n_right, 128), 1) + 128 * part
@@ -78,23 +71,10 @@
     lists[5:8] = jnp.zeros((3, 128), jnp.int32)
 
 
-def prep(wave, picks, left, right):
-    return pl.pallas_call(
-        prep_kernel,
-        out_shape=(
-            jax.ShapeDtypeStruct((16, 2, 128, 128), jnp.bfloat16),
-            jax.ShapeDtypeStruct((8, 128), jnp.int32),
-        ),
-        in_specs=[VMEM, SMEM, VMEM, VMEM],
-        out_specs=(VMEM, VMEM),
-        name="prep",
-    )(wave, picks, left, right)
-
-
 def main_kernel(
-    lists_in, left_in, right_in, outgoing, out,
-    lists_vmem, lists, wave, env, inter, cumulated, partial, parts, result,
-    wrecv, erecv, mate_recv, lists_recv, send, recv, part_send, last_recv, last_send,
+    wave_in, picks, left_in, right_in, left_tasks, right_tasks, out,
+    tiles, outgoing, lists_in, lists_vmem, lists, wave, env, inter, cumulated, partial, parts, result,
+    wrecv, erecv, mate_recv, lists_recv, send, recv, part_send, last_recv, last_send, tiles_recv,
 ):
     z, x, y, c = place()
     xc = 2 * x + c
@@ -105,6 +85,8 @@
     zup, zdown = ((z + 1) % 8, x, y, c), ((z + 7) % 8, x, y, c)
     peers = [(z, (xc + k) % 8 // 2, y, (xc + k) % 8 % 2) for k in range(1, 8)]
 
+    fetch = pltpu.make_async_copy(wave_in, tiles, tiles_recv)
+    fetch.start()
     barrier = pltpu.get_barrier_semaphore()
     for peer in peers + [zup, zdown] + [(z, x, (y + d) % 8, c) for d in range(1, 8)]:
         pl.semaphore_signal(barrier, inc=1, device_id=peer, device_id_type=MESH)
@@ -116,6 +98,14 @@
     wave[128] = jnp.zeros((2, 128, 128), jnp.bfloat16)
     inter[LEFT_PAIRS] = jnp.zeros((2, 128, 128), jnp.bfloat16)
     cumulated[RIGHT_PAIRS] = jnp.zeros((256, 128), jnp.bfloat16)
+    fetch.wait()
+    for to in range(8):
+        owner = (z // 2 * 8 + to) * 2 + z % 2
+        for slot in range(2):
+            index = picks[0, 2 * owner + slot]
+            tile = tiles[jnp.maximum(index, 0)]
+            outgoing[2 * to + slot] = jnp.where(index >= 0, tile, jnp.zeros_like(tile))
+
     pl.semaphore_wait(barrier, 16 + jnp.where(fixed, 0, 1))
     Y_SEND, EY_SEND, MATE_SEND, XUP, XDOWN, ZUP, ZDOWN, E_SEND, LISTS_SEND = range(9)
 
@@ -146,13 +136,11 @@
     def _():
         pltpu.make_async_copy(left_in, env.at[mine, 0], erecv.at[mine]).start()
         pltpu.make_async_copy(right_in, env.at[mine, 1], erecv.at[mine]).start()
-        pltpu.make_async_copy(lists_in, lists_vmem, lists_recv).start()
 
     @pl.when(jnp.logical_not(fixed))
     def _():
         remote(left_in, env.at[mine, 0], E_SEND, erecv.at[mine], partner)
         remote(right_in, env.at[mine, 1], E_SEND, erecv.at[mine], partner)
-        remote(lists_in, lists_vmem, LISTS_SEND, lists_recv, partner)
 
     own = z * 8 + y
 
@@ -175,6 +163,16 @@
     remote(here, chunks(mine), XUP, wrecv.at[mine], xup)
     remote(here, chunks(mine), XDOWN, wrecv.at[mine], xdown)
     remote(here, chunks(mine), MATE_SEND, mate_recv, mate)
+    build_lists(left_tasks, right_tasks, lists_in)
+
+    @pl.when(fixed)
+    def _():
+        pltpu.make_async_copy(lists_in, lists_vmem, lists_recv).start()
+
+    @pl.when(jnp.logical_not(fixed))
+    def _():
+        remote(lists_in, lists_vmem, LISTS_SEND, lists_recv, partner)
+
     wait(env.at[own], erecv.at[own])
     for r in range(1, 5):
         send_env(r)
@@ -319,33 +317,34 @@
         tile = cumulated[lists[4, k]].reshape(2, 8, 16, 128)
         partial[:, k] = jnp.swapaxes(tile, 0, 1)
 
-    def part(k):
-        return pltpu.make_async_remote_copy(
-            src_ref=partial.at[(xc + k) % 8], dst_ref=parts.at[k],
-            send_sem=part_send.at[k], recv_sem=recv.at[k],
-            device_id=peers[k - 1], device_id_type=MESH,
-        )
-
-    copies = [part(k) for k in (1, 7, 2, 6, 3, 5, 4)]
-    for copy in copies:
-        copy.start()
-    for copy in copies:
-        copy.wait_recv()
-    for h in range(2):
-        half = pl.ds(8 * h, 8)
-        total = partial[xc, half].astype(jnp.float32)
+    copies = []
+    for h in range(STEPS):
+        some = pl.ds(TILES // STEPS * h, TILES // STEPS)
+        for k in (4, 5, 3, 6, 2, 7, 1):
+            copy = pltpu.make_async_remote_copy(
+                src_ref=partial.at[(xc + k) % 8, some], dst_ref=parts.at[k, some],
+                send_sem=part_send.at[8 * h + k], recv_sem=recv.at[8 * h + k],
+                device_id=peers[k - 1], device_id_type=MESH,
+            )
+            copy.start()
+            copies.append(copy)
+    for h in range(STEPS):
+        some = pl.ds(TILES // STEPS * h, TILES // STEPS)
+        for copy in copies[7 * h : 7 * h + 7]:
+            copy.wait_recv()
+        total = partial[xc, some].astype(jnp.float32)
         for k in range(1, 8):
-            total += parts[k, half].astype(jnp.float32)
-        result[half] = total.astype(jnp.bfloat16)
+            total += parts[k, some].astype(jnp.float32)
+        result[some] = total.astype(jnp.bfloat16)
 
         @pl.when(fixed)
         def _():
-            pltpu.make_async_copy(result.at[half], out.at[half], last_recv.at[h]).start()
+            pltpu.make_async_copy(result.at[some], out.at[some], last_recv.at[h]).start()
 
         @pl.when(jnp.logical_not(fixed))
         def _():
             pltpu.make_async_remote_copy(
-                src_ref=result.at[half], dst_ref=out.at[half],
+                src_ref=result.at[some], dst_ref=out.at[some],
                 send_sem=last_send.at[h], recv_sem=last_recv.at[h],
                 device_id=partner, device_id_type=MESH,
             ).start()
@@ -364,20 +363,23 @@
     def _():
         wait(env.at[0], send.at[E_SEND])
         wait(lists_vmem, send.at[LISTS_SEND])
-        for h in range(2):
-            wait(result.at[pl.ds(8 * h, 8)], last_send.at[h])
-
-    for h in range(2):
-        wait(result.at[pl.ds(8 * h, 8)], last_recv.at[h])
-
-
-def main(lists, left, right, outgoing):
+        for h in range(STEPS):
+            wait(result.at[pl.ds(0, TILES // STEPS)], last_send.at[h])
+
+    for h in range(STEPS):
+        wait(result.at[pl.ds(0, TILES // STEPS)], last_recv.at[h])
+
+
+def main(*operands):
     return pl.pallas_call(
         main_kernel,
         out_shape=jax.ShapeDtypeStruct((TILES, 2, 16, 128), jnp.bfloat16),
-        in_specs=[VMEM, ANY, ANY, VMEM],
+        in_specs=[ANY, SMEM, ANY, ANY, VMEM, VMEM],
         out_specs=VMEM,
         scratch_shapes=[
+            pltpu.VMEM((16, 2, 128, 128), jnp.bfloat16),
+            pltpu.VMEM((16, 2, 128, 128), jnp.bfloat16),
+            pltpu.VMEM((8, 128), jnp.int32),
             pltpu.VMEM((8, 128), jnp.int32),
             pltpu.SMEM((8, 128), jnp.int32),
             pltpu.VMEM((129, 2, 128, 128), jnp.bfloat16),
@@ -392,21 +394,28 @@
             pltpu.SemaphoreType.DMA,
             pltpu.SemaphoreType.DMA,
             pltpu.SemaphoreType.DMA((9,)),
-            pltpu.SemaphoreType.DMA((8,)),
-            pltpu.SemaphoreType.DMA((8,)),
-            pltpu.SemaphoreType.DMA((2,)),
-            pltpu.SemaphoreType.DMA((2,)),
+            pltpu.SemaphoreType.DMA((8 * STEPS,)),
+            pltpu.SemaphoreType.DMA((8 * STEPS,)),
+            pltpu.SemaphoreType.DMA((STEPS,)),
+            pltpu.SemaphoreType.DMA((STEPS,)),
+            pltpu.SemaphoreType.DMA,
         ],
         compiler_params=pltpu.CompilerParams(
-            collective_id=0, has_side_effects=True, vmem_limit_bytes=44 << 20
+            collective_id=0, has_side_effects=True, vmem_limit_bytes=60 << 20
         ),
         name="main",
-    )(lists, left, right, outgoing)
+    )(*operands)
 
 
 def shards(wave_tiles, left_env, right_env, send_list, left_tasks, right_tasks):
-    outgoing, lists = prep(wave_tiles, send_list, left_tasks[0, 0].T, right_tasks[0, 0].T)
-    rows = main(lists, left_env[0, 0], right_env[0, 0], outgoing)
+    rows = main(
+        wave_tiles,
+        send_list,
+        left_env[0, 0],
+        right_env[0, 0],
+        jnp.transpose(left_tasks[0], (2, 0, 1)),
+        jnp.transpose(right_tasks[0], (2, 0, 1)),
+    )
     return rows.astype(jnp.float32)
 
 

time: 114 us -> 105 us (0.921)
  the two profiles are of different devices: /device:TPU:10 before, /device:TPU:5 now
where the time goes in v4:
time: 105 us
  Pallas kernels  103 us (98%)
  other arithmetic  1.63 us (2%)
    pallas_call x1, Pallas kernels, main(): pl.pallas_call(main_kernel, out_shape=jax.ShapeDtypeStruct((TILES, 2, 16,...  103 us

profile of v4, /device:TPU:5, one launch (start us, length us, event | category | flops | bytes accessed | tf_op | source)
XLA Modules:
  0.0 104.6 jit_solution(451478753987520669)
XLA Ops:
  0.0 103.0 %main.1 = bf16[16,2,16,128]{3,2,1,0:T(8,128)(2,1)} custom-call(bf16[16,2,128,128]{3,2,1,0:T(8,128)(2,1)} %wave_in.1, s32[1,128]{1,0:T(1,128)} %picks.1, bf16[128,128]{1,0:T(8,128)(2,1)} %bitcast.8, bf16[128,128]{1,0:T(8,128)(2,1)} %bitcast.9, s32[3,1,96]{2,1,0:T(1,128)} %bitcast.11, s32[3,1,256]{2,1,0:T(1,128)} %bitcast.10), custom_call_target="tpu_custom_call" | custom-call | tf_op jit(solution)/shard_map/main/pallas_call | solution.py:374
  103.0 1.6 %convert_element_type.3 = f32[16,2,16,128]{3,2,1,0:T(8,128)} convert(bf16[16,2,16,128]{3,2,1,0:T(8,128)(2,1)} %main.1) | non-fusion elementwise | flops 65536 | bytes 393216 | tf_op jit(solution)/shard_map/convert_element_type | solution.py:419

commit v5 on v4

--- a/solution.py
+++ b/solution.py
@@ -73,8 +73,10 @@
 
 def main_kernel(
     wave_in, picks, left_in, right_in, left_tasks, right_tasks, out,
-    tiles, outgoing, lists_in, lists_vmem, lists, wave, env, inter, cumulated, partial, parts, result,
-    wrecv, erecv, mate_recv, lists_recv, send, recv, part_send, last_recv, last_send, tiles_recv,
+    tiles, outgoing, lists_in, lists_vmem, lists, wave, env, inter,
+    cumulated, partial, theirs, pair, parts, result,
+    wrecv, erecv, mate_recv, lists_recv, send, theirs_recv, theirs_send,
+    recv, part_send, last_recv, last_send, tiles_recv,
 ):
     z, x, y, c = place()
     xc = 2 * x + c
@@ -83,12 +85,12 @@
     mate = (z, x, y, 1 - c)
     xup, xdown = (z, (x + 1) % 4, y, c), (z, (x + 3) % 4, y, c)
     zup, zdown = ((z + 1) % 8, x, y, c), ((z + 7) % 8, x, y, c)
-    peers = [(z, (xc + k) % 8 // 2, y, (xc + k) % 8 % 2) for k in range(1, 8)]
+    lane = [(z, (x + k) % 4, y, c) for k in range(1, 4)]
 
     fetch = pltpu.make_async_copy(wave_in, tiles, tiles_recv)
     fetch.start()
     barrier = pltpu.get_barrier_semaphore()
-    for peer in peers + [zup, zdown] + [(z, x, (y + d) % 8, c) for d in range(1, 8)]:
+    for peer in lane + [mate, zup, zdown] + [(z, x, (y + d) % 8, c) for d in range(1, 8)]:
         pl.semaphore_signal(barrier, inc=1, device_id=peer, device_id_type=MESH)
 
     @pl.when(jnp.logical_not(fixed))
@@ -97,7 +99,7 @@
 
     wave[128] = jnp.zeros((2, 128, 128), jnp.bfloat16)
     inter[LEFT_PAIRS] = jnp.zeros((2, 128, 128), jnp.bfloat16)
-    cumulated[RIGHT_PAIRS] = jnp.zeros((256, 128), jnp.bfloat16)
+    cumulated[RIGHT_PAIRS] = jnp.zeros((256, 128), jnp.float32)
     fetch.wait()
     for to in range(8):
         owner = (z // 2 * 8 + to) * 2 + z % 2
@@ -106,7 +108,7 @@
             tile = tiles[jnp.maximum(index, 0)]
             outgoing[2 * to + slot] = jnp.where(index >= 0, tile, jnp.zeros_like(tile))
 
-    pl.semaphore_wait(barrier, 16 + jnp.where(fixed, 0, 1))
+    pl.semaphore_wait(barrier, 13 + jnp.where(fixed, 0, 1))
     Y_SEND, EY_SEND, MATE_SEND, XUP, XDOWN, ZUP, ZDOWN, E_SEND, LISTS_SEND = range(9)
 
     def remote(source, target, sender, receiver, device):
@@ -294,7 +296,7 @@
         inter[p, 1] = total[:, 128:].astype(jnp.bfloat16)
         return total
 
-    lax.fori_loop(0, LEFT_PAIRS, left_pair, jnp.zeros((128, 256), jnp.float32), unroll=8)
+    lax.fori_loop(0, LEFT_PAIRS, left_pair, jnp.zeros((128, 256), jnp.float32), unroll=16)
 
     def right_pair(p, total):
         row, column = 1 + p // 64, 2 * (p % 64)
@@ -309,42 +311,54 @@
         rhs = jnp.concatenate([env[one & 63, 1], env[two & 63, 1]], axis=0)
         product = jnp.dot(lhs, rhs, preferred_element_type=jnp.float32)
         total = product + total * (one >> 16).astype(jnp.float32)
-        cumulated[p] = total.astype(jnp.bfloat16)
+        cumulated[p] = total
         return total
 
-    lax.fori_loop(0, RIGHT_PAIRS, right_pair, jnp.zeros((256, 128), jnp.float32), unroll=8)
-    for k in range(TILES):
-        tile = cumulated[lists[4, k]].reshape(2, 8, 16, 128)
-        partial[:, k] = jnp.swapaxes(tile, 0, 1)
-
-    copies = []
+    lax.fori_loop(0, RIGHT_PAIRS, right_pair, jnp.zeros((256, 128), jnp.float32), unroll=17)
+
+    def block(h):
+        return pl.ds(TILES // STEPS * h, TILES // STEPS)
+
+    def to_mate(h):
+        return pltpu.make_async_remote_copy(
+            src_ref=partial.at[1 - c, :, block(h)], dst_ref=theirs.at[:, block(h)],
+            send_sem=theirs_send.at[h], recv_sem=theirs_recv.at[h],
+            device_id=mate, device_id_type=MESH,
+        )
+
+    def to_chip(h, k):
+        return pltpu.make_async_remote_copy(
+            src_ref=pair.at[(x + k) % 4, block(h)], dst_ref=parts.at[k - 1, block(h)],
+            send_sem=part_send.at[4 * h + k], recv_sem=recv.at[4 * h + k],
+            device_id=lane[k - 1], device_id_type=MESH,
+        )
+
     for h in range(STEPS):
-        some = pl.ds(TILES // STEPS * h, TILES // STEPS)
-        for k in (4, 5, 3, 6, 2, 7, 1):
-            copy = pltpu.make_async_remote_copy(
-                src_ref=partial.at[(xc + k) % 8, some], dst_ref=parts.at[k, some],
-                send_sem=part_send.at[8 * h + k], recv_sem=recv.at[8 * h + k],
-                device_id=peers[k - 1], device_id_type=MESH,
-            )
-            copy.start()
-            copies.append(copy)
+        for k in range(TILES // STEPS * h, TILES // STEPS * (h + 1)):
+            tile = cumulated[lists[4, k]].reshape(2, 8, 16, 128)
+            for t in range(8):
+                partial[t % 2, t // 2, k] = tile[:, t]
+        to_mate(h).start()
     for h in range(STEPS):
-        some = pl.ds(TILES // STEPS * h, TILES // STEPS)
-        for copy in copies[7 * h : 7 * h + 7]:
-            copy.wait_recv()
-        total = partial[xc, some].astype(jnp.float32)
-        for k in range(1, 8):
-            total += parts[k, some].astype(jnp.float32)
-        result[some] = total.astype(jnp.bfloat16)
+        to_mate(h).wait_recv()
+        pair[:, block(h)] = (partial[c, :, block(h)] + theirs[:, block(h)]).astype(jnp.bfloat16)
+        for k in (2, 1, 3):
+            to_chip(h, k).start()
+    for h in range(STEPS):
+        total = partial[c, x, block(h)] + theirs[x, block(h)]
+        for k in (1, 2, 3):
+            to_chip(h, k).wait_recv()
+            total += parts[k - 1, block(h)].astype(jnp.float32)
+        result[block(h)] = total.astype(jnp.bfloat16)
 
         @pl.when(fixed)
         def _():
-            pltpu.make_async_copy(result.at[some], out.at[some], last_recv.at[h]).start()
+            pltpu.make_async_copy(result.at[block(h)], out.at[block(h)], last_recv.at[h]).start()
 
         @pl.when(jnp.logical_not(fixed))
         def _():
             pltpu.make_async_remote_copy(
-                src_ref=result.at[some], dst_ref=out.at[some],
+                src_ref=result.at[block(h)], dst_ref=out.at[block(h)],
                 send_sem=last_send.at[h], recv_sem=last_recv.at[h],
                 device_id=partner, device_id_type=MESH,
             ).start()
@@ -356,8 +370,10 @@
     wait(chunks(0, 12), send.at[XDOWN])
     wait(env.at[pl.ds(0, 28)], send.at[ZUP])
     wait(env.at[pl.ds(0, 28)], send.at[ZDOWN])
-    for copy in copies:
-        copy.wait_send()
+    for h in range(STEPS):
+        to_mate(h).wait_send()
+        for k in (1, 2, 3):
+            to_chip(h, k).wait_send()
 
     @pl.when(jnp.logical_not(fixed))
     def _():
@@ -385,17 +401,21 @@
             pltpu.VMEM((129, 2, 128, 128), jnp.bfloat16),
             pltpu.VMEM((64, 2, 128, 128), jnp.bfloat16),
             pltpu.VMEM((LEFT_PAIRS + 1, 2, 128, 128), jnp.bfloat16),
-            pltpu.VMEM((RIGHT_PAIRS + 1, 256, 128), jnp.bfloat16),
-            pltpu.VMEM((8, TILES, 2, 16, 128), jnp.bfloat16),
-            pltpu.VMEM((8, TILES, 2, 16, 128), jnp.bfloat16),
+            pltpu.VMEM((RIGHT_PAIRS + 1, 256, 128), jnp.float32),
+            pltpu.VMEM((2, 4, TILES, 2, 16, 128), jnp.float32),
+            pltpu.VMEM((4, TILES, 2, 16, 128), jnp.float32),
+            pltpu.VMEM((4, TILES, 2, 16, 128), jnp.bfloat16),
+            pltpu.VMEM((3, TILES, 2, 16, 128), jnp.bfloat16),
             pltpu.VMEM((TILES, 2, 16, 128), jnp.bfloat16),
             pltpu.SemaphoreType.DMA((64,)),
             pltpu.SemaphoreType.DMA((64,)),
             pltpu.SemaphoreType.DMA,
             pltpu.SemaphoreType.DMA,
             pltpu.SemaphoreType.DMA((9,)),
-            pltpu.SemaphoreType.DMA((8 * STEPS,)),
-            pltpu.SemaphoreType.DMA((8 * STEPS,)),
+            pltpu.SemaphoreType.DMA((STEPS,)),
+            pltpu.SemaphoreType.DMA((STEPS,)),
+            pltpu.SemaphoreType.DMA((4 * STEPS,)),
+            pltpu.SemaphoreType.DMA((4 * STEPS,)),
             pltpu.SemaphoreType.DMA((STEPS,)),
             pltpu.SemaphoreType.DMA((STEPS,)),
             pltpu.SemaphoreType.DMA,

time: 105 us -> 100 us (0.952)
  the two profiles are of different devices: /device:TPU:5 before, /device:TPU:10 now
where the time goes in v5:
time: 100 us
  Pallas kernels  98.4 us (98%)
  other arithmetic  1.63 us (2%)
    pallas_call x1, Pallas kernels, main(): pl.pallas_call(main_kernel, out_shape=jax.ShapeDtypeStruct((TILES, 2, 16,...  98.4 us

profile of v5, /device:TPU:10, one launch (start us, length us, event | category | flops | bytes accessed | tf_op | source)
XLA Modules:
  0.0 100.0 jit_solution(8284542963098942001)
XLA Ops:
  0.0 98.4 %main.1 = bf16[16,2,16,128]{3,2,1,0:T(8,128)(2,1)} custom-call(bf16[16,2,128,128]{3,2,1,0:T(8,128)(2,1)} %wave_in.1, s32[1,128]{1,0:T(1,128)} %picks.1, bf16[128,128]{1,0:T(8,128)(2,1)} %bitcast.8, bf16[128,128]{1,0:T(8,128)(2,1)} %bitcast.9, s32[3,1,96]{2,1,0:T(1,128)} %bitcast.11, s32[3,1,256]{2,1,0:T(1,128)} %bitcast.10), custom_call_target="tpu_custom_call" | custom-call | tf_op jit(solution)/shard_map/main/pallas_call | solution.py:390
  98.4 1.6 %convert_element_type.3 = f32[16,2,16,128]{3,2,1,0:T(8,128)} convert(bf16[16,2,16,128]{3,2,1,0:T(8,128)(2,1)} %main.1) | non-fusion elementwise | flops 65536 | bytes 393216 | tf_op jit(solution)/shard_map/convert_element_type | solution.py:439

commit v6 on v5

--- a/solution.py
+++ b/solution.py
@@ -185,8 +185,8 @@
     def turn(i, carry):
         @pl.when(i < 3)
         def _():
+            send_wave(i + 5)
             send_env(i + 5)
-            send_wave(i + 5)
 
         @pl.when(i < 8)
         def _():
@@ -296,7 +296,7 @@
         inter[p, 1] = total[:, 128:].astype(jnp.bfloat16)
         return total
 
-    lax.fori_loop(0, LEFT_PAIRS, left_pair, jnp.zeros((128, 256), jnp.float32), unroll=16)
+    lax.fori_loop(0, LEFT_PAIRS, left_pair, jnp.zeros((128, 256), jnp.float32), unroll=32)
 
     def right_pair(p, total):
         row, column = 1 + p // 64, 2 * (p % 64)
@@ -314,7 +314,7 @@
         cumulated[p] = total
         return total
 
-    lax.fori_loop(0, RIGHT_PAIRS, right_pair, jnp.zeros((256, 128), jnp.float32), unroll=17)
+    lax.fori_loop(0, RIGHT_PAIRS, right_pair, jnp.zeros((256, 128), jnp.float32), unroll=34)
 
     def block(h):
         return pl.ds(TILES // STEPS * h, TILES // STEPS)

time: 100 us -> 98.7 us (0.987)
  the two profiles are of different devices: /device:TPU:10 before, /device:TPU:7 now
where the time goes in v6:
time: 98.7 us; the launch traced here: 97.2 us
  Pallas kernels  95.6 us (97%)
  other arithmetic  1.63 us (2%)
    pallas_call x1, Pallas kernels, main(): pl.pallas_call(main_kernel, out_shape=jax.ShapeDtypeStruct((TILES, 2, 16,...  95.6 us

profile of v6, /device:TPU:7, one launch (start us, length us, event | category | flops | bytes accessed | tf_op | source)
XLA Modules:
  0.0 97.2 jit_solution(5391247789801507765)
XLA Ops:
  0.0 95.6 %main.1 = bf16[16,2,16,128]{3,2,1,0:T(8,128)(2,1)} custom-call(bf16[16,2,128,128]{3,2,1,0:T(8,128)(2,1)} %wave_in.1, s32[1,128]{1,0:T(1,128)} %picks.1, bf16[128,128]{1,0:T(8,128)(2,1)} %bitcast.8, bf16[128,128]{1,0:T(8,128)(2,1)} %bitcast.9, s32[3,1,96]{2,1,0:T(1,128)} %bitcast.11, s32[3,1,256]{2,1,0:T(1,128)} %bitcast.10), custom_call_target="tpu_custom_call" | custom-call | tf_op jit(solution)/shard_map/main/pallas_call | solution.py:390
  95.6 1.6 %convert_element_type.3 = f32[16,2,16,128]{3,2,1,0:T(8,128)} convert(bf16[16,2,16,128]{3,2,1,0:T(8,128)(2,1)} %main.1) | non-fusion elementwise | flops 65536 | bytes 393216 | tf_op jit(solution)/shard_map/convert_element_type | solution.py:439

commit v7 on v6

--- a/solution.py
+++ b/solution.py
@@ -100,6 +100,42 @@
     wave[128] = jnp.zeros((2, 128, 128), jnp.bfloat16)
     inter[LEFT_PAIRS] = jnp.zeros((2, 128, 128), jnp.bfloat16)
     cumulated[RIGHT_PAIRS] = jnp.zeros((256, 128), jnp.float32)
+    pl.semaphore_wait(barrier, 13 + jnp.where(fixed, 0, 1))
+    Y_SEND, EY_SEND, MATE_SEND, XUP, XDOWN, ZUP, ZDOWN, E_SEND, LISTS_SEND = range(9)
+
+    def remote(source, target, sender, receiver, device):
+        pltpu.make_async_remote_copy(
+            src_ref=source, dst_ref=target, send_sem=send.at[sender], recv_sem=receiver,
+            device_id=device, device_id_type=MESH,
+        ).start()
+
+    def wait(ref, sem):
+        pltpu.make_async_copy(ref, ref, sem).wait()
+
+    def chunks(slot, count=1):
+        return wave.at[pl.ds(2 * slot, 2 * count)]
+
+    def pass_wave(slot, sender, device):
+        remote(chunks(slot), chunks(slot), sender, wrecv.at[slot], device)
+
+    def pass_mate(slot):
+        remote(chunks(slot), chunks(slot), MATE_SEND, mate_recv, mate)
+
+    def pass_env(slot, sender, device):
+        remote(env.at[slot], env.at[slot], sender, erecv.at[slot], device)
+
+    mine = xc * 8 + y
+
+    @pl.when(fixed)
+    def _():
+        pltpu.make_async_copy(left_in, env.at[mine, 0], erecv.at[mine]).start()
+        pltpu.make_async_copy(right_in, env.at[mine, 1], erecv.at[mine]).start()
+
+    @pl.when(jnp.logical_not(fixed))
+    def _():
+        remote(left_in, env.at[mine, 0], E_SEND, erecv.at[mine], partner)
+        remote(right_in, env.at[mine, 1], E_SEND, erecv.at[mine], partner)
+
     fetch.wait()
     for to in range(8):
         owner = (z // 2 * 8 + to) * 2 + z % 2
@@ -107,42 +143,6 @@
             index = picks[0, 2 * owner + slot]
             tile = tiles[jnp.maximum(index, 0)]
             outgoing[2 * to + slot] = jnp.where(index >= 0, tile, jnp.zeros_like(tile))
-
-    pl.semaphore_wait(barrier, 13 + jnp.where(fixed, 0, 1))
-    Y_SEND, EY_SEND, MATE_SEND, XUP, XDOWN, ZUP, ZDOWN, E_SEND, LISTS_SEND = range(9)
-
-    def remote(source, target, sender, receiver, device):
-        pltpu.make_async_remote_copy(
-            src_ref=source, dst_ref=target, send_sem=send.at[sender], recv_sem=receiver,
-            device_id=device, device_id_type=MESH,
-        ).start()
-
-    def wait(ref, sem):
-        pltpu.make_async_copy(ref, ref, sem).wait()
-
-    def chunks(slot, count=1):
-        return wave.at[pl.ds(2 * slot, 2 * count)]
-
-    def pass_wave(slot, sender, device):
-        remote(chunks(slot), chunks(slot), sender, wrecv.at[slot], device)
-
-    def pass_mate(slot):
-        remote(chunks(slot), chunks(slot), MATE_SEND, mate_recv, mate)
-
-    def pass_env(slot, sender, device):
-        remote(env.at[slot], env.at[slot], sender, erecv.at[slot], device)
-
-    mine = xc * 8 + y
-
-    @pl.when(fixed)
-    def _():
-        pltpu.make_async_copy(left_in, env.at[mine, 0], erecv.at[mine]).start()
-        pltpu.make_async_copy(right_in, env.at[mine, 1], erecv.at[mine]).start()
-
-    @pl.when(jnp.logical_not(fixed))
-    def _():
-        remote(left_in, env.at[mine, 0], E_SEND, erecv.at[mine], partner)
-        remote(right_in, env.at[mine, 1], E_SEND, erecv.at[mine], partner)
 
     own = z * 8 + y
 

time: 98.7 us -> 98.9 us (level)
  no operation moved by 1% of the time
where the time goes in v7:
time: 98.9 us; the launch traced here: 97.8 us
  Pallas kernels  96.2 us (97%)
  other arithmetic  1.63 us (2%)
    pallas_call x1, Pallas kernels, main(): pl.pallas_call(main_kernel, out_shape=jax.ShapeDtypeStruct((TILES, 2, 16,...  96.2 us

profile of v7, /device:TPU:7, one launch (start us, length us, event | category | flops | bytes accessed | tf_op | source)
XLA Modules:
  0.0 97.8 jit_solution(16639452598623110147)
XLA Ops:
  0.0 96.2 %main.1 = bf16[16,2,16,128]{3,2,1,0:T(8,128)(2,1)} custom-call(bf16[16,2,128,128]{3,2,1,0:T(8,128)(2,1)} %wave_in.1, s32[1,128]{1,0:T(1,128)} %picks.1, bf16[128,128]{1,0:T(8,128)(2,1)} %bitcast.8, bf16[128,128]{1,0:T(8,128)(2,1)} %bitcast.9, s32[3,1,96]{2,1,0:T(1,128)} %bitcast.11, s32[3,1,256]{2,1,0:T(1,128)} %bitcast.10), custom_call_target="tpu_custom_call" | custom-call | tf_op jit(solution)/shard_map/main/pallas_call | solution.py:390
  96.2 1.6 %convert_element_type.3 = f32[16,2,16,128]{3,2,1,0:T(8,128)} convert(bf16[16,2,16,128]{3,2,1,0:T(8,128)(2,1)} %main.1) | non-fusion elementwise | flops 65536 | bytes 393216 | tf_op jit(solution)/shard_map/convert_element_type | solution.py:439
